TPU v7x, 32 devices: a whole 2x2x4 slice. The times are simulated.
32 devices in a mesh: ctx: 8 (over y, x, core), tp: 4 (over z).
Axes of the slice: x: 2, y: 2, z: 4, core: 2. Of those that a mesh axis runs over, the one named last changes fastest.
Arguments:
- layer_input: bfloat16 [4096, 5120], P('ctx', 'tp'), may hold values from -6 to 6
- w_query: bfloat16 [5120, 5120], P(None, 'tp'), may hold values from -0.078125 to 0.078125
- w_key: bfloat16 [5120, 1024], P(None, 'tp'), may hold values from -0.078125 to 0.078125
- w_value: bfloat16 [5120, 1024], P(None, 'tp'), may hold values from -0.078125 to 0.078125
- queries: bfloat16 [4096, 5120], P('ctx', 'tp'), may hold values from -40 to 40
- keys: bfloat16 [4096, 1024], P('ctx', 'tp'), may hold values from -4 to 4
- values: bfloat16 [4096, 1024], P('ctx', 'tp'), may hold values from -6 to 6
- grad_out: bfloat16 [4096, 5120], P('ctx', 'tp'), may hold values from -1.5 to 1.5
- block_lists: int32 [32, 6], P('ctx'), may hold values from -1 to 31, as said below
- global_ids: int32 [2], replicated, may hold values from 0 to 15, as said below
Outputs:
- grad_x: bfloat16 [4096, 5120], P('ctx', 'tp')
- grad_w_query: bfloat16 [5120, 5120], P('ctx', 'tp')
- grad_w_key: bfloat16 [5120, 1024], P('ctx', 'tp')
- grad_w_value: bfloat16 [5120, 1024], P('ctx', 'tp')
Inputs may be any that keep to these rules, and one draw needn't show every extreme that they name: `global_ids`: 2 distinct blocks of the first half of the sequence; the last block of the first half is always one of them. `block_lists`: row a lists distinct key blocks b <= a that are not global, -1 for an empty slot: block a itself, a - 1 and a - 2 where they exist and are not global, then blocks drawn at random below a.
All inputs are finite; a program needn't handle non-finite values.
Results may differ from a plain program's by a relative error of at most 0.025.
Values may be sent and summed in bfloat16 or wider, within the bound.
No kernel may reach another device: no remote copies, remote signals or barrier semaphores. Data moves between devices by JAX's collectives and lax.ppermute only.
A program may use at most 192 MiB of HBM per device.

v0:
```python
import math

import jax
import jax.numpy as jnp
from jax import lax
from jax.sharding import PartitionSpec as P

H = 40
KVH = 8
HD = 128
BLK = 128
NGLOB = 2


masked_score = -1e30


def sparse_grads(query_blk, dout_blk, key_sel, value_sel, keep_mask, score_scale):
    scores = (
        jnp.einsum("ithgd,isuhd->ihgtsu", query_blk, key_sel, preferred_element_type=jnp.float32)
        * score_scale
    )
    scores = jnp.where(keep_mask, scores, masked_score)
    row_top = jnp.max(scores, axis=(4, 5), keepdims=True)
    row_total = jnp.sum(
        jnp.where(keep_mask, jnp.exp(scores - row_top), 0.0), axis=(4, 5), keepdims=True
    )
    prob_f32 = jnp.where(keep_mask, jnp.exp(scores - (row_top + jnp.log(row_total))), 0.0)
    prob_b = prob_f32.astype(jnp.bfloat16)
    output = jnp.einsum(
        "ihgtsu,isuhd->ithgd", prob_b, value_sel, preferred_element_type=jnp.float32
    )
    delta = jnp.sum(dout_blk.astype(jnp.float32) * output, axis=-1)
    delta = jnp.transpose(delta, (0, 2, 3, 1))[..., None, None]
    dprob = jnp.einsum(
        "ithgd,isuhd->ihgtsu", dout_blk, value_sel, preferred_element_type=jnp.float32
    )
    dscore = (prob_f32 * (dprob - delta) * score_scale).astype(jnp.bfloat16)
    query_grad = jnp.einsum(
        "ihgtsu,isuhd->ithgd", dscore, key_sel, preferred_element_type=jnp.float32
    )
    key_grad = jnp.einsum(
        "ihgtsu,ithgd->isuhd", dscore, query_blk, preferred_element_type=jnp.float32
    )
    value_grad = jnp.einsum(
        "ihgtsu,ithgd->isuhd", prob_b, dout_blk, preferred_element_type=jnp.float32
    )
    return (query_grad, key_grad, value_grad)


def dense_scores(query_rows, key_rows, keep_mask, score_scale):
    scores = (
        jnp.einsum("thgd,uhd->hgtu", query_rows, key_rows, preferred_element_type=jnp.float32)
        * score_scale
    )
    return jnp.where(keep_mask, scores, masked_score)


def dense_stats(scores, keep_mask):
    row_top = jnp.max(scores, axis=-1, keepdims=True)
    row_total = jnp.sum(
        jnp.where(keep_mask, jnp.exp(scores - row_top), 0.0), axis=-1, keepdims=True
    )
    return (row_top, row_total)


def dense_probs(scores, keep_mask, row_top, row_total):
    return jnp.where(keep_mask, jnp.exp(scores - (row_top + jnp.log(row_total))), 0.0)


def dense_back(query_rows, dout_rows, key_rows, value_rows, prob_f32, prob_b, output, score_scale):
    delta = jnp.sum(dout_rows.astype(jnp.float32) * output, axis=-1)
    delta = jnp.transpose(delta, (1, 2, 0))[..., None]
    dprob = jnp.einsum("thgd,uhd->hgtu", dout_rows, value_rows, preferred_element_type=jnp.float32)
    dscore = (prob_f32 * (dprob - delta) * score_scale).astype(jnp.bfloat16)
    query_grad = jnp.einsum("hgtu,uhd->thgd", dscore, key_rows, preferred_element_type=jnp.float32)
    key_grad = jnp.einsum("hgtu,thgd->uhd", dscore, query_rows, preferred_element_type=jnp.float32)
    value_grad = jnp.einsum("hgtu,thgd->uhd", prob_b, dout_rows, preferred_element_type=jnp.float32)
    return (query_grad, key_grad, value_grad)


def add_rows(target, row_start, addition):
    current = lax.dynamic_slice_in_dim(target, row_start, addition.shape[0], 0)
    return lax.dynamic_update_slice_in_dim(target, current + addition, row_start, 0)


def shards(
    layer_input, w_query, w_key, w_value, queries, keys, values, grad_out, block_lists, global_ids
):
    tok_rows = queries.shape[0]
    blk_count = tok_rows // BLK
    kv_heads = keys.shape[1] // HD
    groups = H // KVH
    score_scale = 1.0 / math.sqrt(HD)
    ctx_size = lax.axis_size("ctx")
    ctx_pos = lax.axis_index("ctx")
    total_blocks = blk_count * ctx_size
    total_rows = total_blocks * BLK
    first_block = ctx_pos * blk_count
    own_blocks = first_block + jnp.arange(blk_count, dtype=jnp.int32)
    key_all, value_all = (
        lax.all_gather(keys, "ctx", axis=0, tiled=True),
        lax.all_gather(values, "ctx", axis=0, tiled=True),
    )
    key_blocks = key_all.reshape(total_blocks, BLK, kv_heads, HD)
    value_blocks = value_all.reshape(total_blocks, BLK, kv_heads, HD)
    query_blk = queries.reshape(blk_count, BLK, kv_heads, groups, HD)
    dout_blk = grad_out.reshape(blk_count, BLK, kv_heads, groups, HD)
    is_global = jnp.any(own_blocks[:, None] == global_ids[None, :], axis=1)
    slot_ids = jnp.concatenate(
        [jnp.maximum(block_lists, 0), jnp.broadcast_to(global_ids[None, :], (blk_count, NGLOB))],
        axis=1,
    )
    usable = (
        jnp.concatenate([block_lists >= 0, global_ids[None, :] <= own_blocks[:, None]], axis=1)
        & ~is_global[:, None]
    )
    causal = jnp.arange(BLK, dtype=jnp.int32)[None, :] <= jnp.arange(BLK, dtype=jnp.int32)[:, None]
    diagonal = slot_ids == own_blocks[:, None]
    keep_mask = usable[:, None, None, None, :, None] & (
        (~diagonal)[:, None, None, None, :, None] | causal[None, None, None, :, None, :]
    )
    key_sel = key_blocks[slot_ids]
    value_sel = value_blocks[slot_ids]
    query_grad, key_sel_grad, value_sel_grad = sparse_grads(
        query_blk, dout_blk, key_sel, value_sel, keep_mask, score_scale
    )
    flat_slots = slot_ids.reshape(-1)
    key_grad_all = (
        jnp.zeros((total_blocks, BLK, kv_heads, HD), jnp.float32)
        .at[flat_slots]
        .add(key_sel_grad.reshape(-1, BLK, kv_heads, HD))
    )
    value_grad_all = (
        jnp.zeros((total_blocks, BLK, kv_heads, HD), jnp.float32)
        .at[flat_slots]
        .add(value_sel_grad.reshape(-1, BLK, kv_heads, HD))
    )
    key_grad_all = key_grad_all.reshape(total_rows, kv_heads, HD)
    value_grad_all = value_grad_all.reshape(total_rows, kv_heads, HD)
    query_grad = query_grad.reshape(tok_rows, kv_heads, groups, HD)
    query_flat = queries.reshape(tok_rows, kv_heads, groups, HD)
    dout_flat = grad_out.reshape(tok_rows, kv_heads, groups, HD)
    row_offsets = jnp.arange(BLK, dtype=jnp.int32)[:, None]
    front_rows = total_blocks // 2 * BLK
    key_front = key_all[:front_rows].reshape(front_rows, kv_heads, HD)
    value_front = value_all[:front_rows].reshape(front_rows, kv_heads, HD)
    front_pos = jnp.arange(front_rows, dtype=jnp.int32)
    for global_num in range(NGLOB):
        global_blk = global_ids[global_num]
        is_mine = (global_blk >= first_block) & (global_blk < first_block + blk_count)
        row_start = jnp.clip(global_blk - first_block, 0, blk_count - 1) * BLK

        def owned(row_start=row_start, global_blk=global_blk):
            query_rows = lax.dynamic_slice_in_dim(query_flat, row_start, BLK, 0)
            dout_rows = lax.dynamic_slice_in_dim(dout_flat, row_start, BLK, 0)
            dense_mask = (front_pos[None, :] <= global_blk * BLK + row_offsets)[None, None]
            scores = dense_scores(query_rows, key_front, dense_mask, score_scale)
            row_top, row_total = dense_stats(scores, dense_mask)
            prob_f32 = dense_probs(scores, dense_mask, row_top, row_total)
            prob_b = prob_f32.astype(jnp.bfloat16)
            output = jnp.einsum(
                "hgtu,uhd->thgd", prob_b, value_front, preferred_element_type=jnp.float32
            )
            return dense_back(
                query_rows, dout_rows, key_front, value_front, prob_f32, prob_b, output, score_scale
            )

        def skipped():
            return (
                jnp.zeros((BLK, kv_heads, groups, HD), jnp.float32),
                jnp.zeros((front_rows, kv_heads, HD), jnp.float32),
                jnp.zeros((front_rows, kv_heads, HD), jnp.float32),
            )

        query_part, key_part, value_part = lax.cond(is_mine, owned, skipped)
        query_grad = add_rows(query_grad, row_start, query_part)
        key_grad_all = key_grad_all.at[:front_rows].add(key_part)
        value_grad_all = value_grad_all.at[:front_rows].add(value_part)
    key_cols_all = kv_heads * HD
    key_local, value_local = (
        lax.psum_scatter(
            key_grad_all.reshape(total_rows, key_cols_all).astype(jnp.bfloat16),
            "ctx",
            scatter_dimension=0,
            tiled=True,
        ).astype(jnp.float32),
        lax.psum_scatter(
            value_grad_all.reshape(total_rows, key_cols_all).astype(jnp.bfloat16),
            "ctx",
            scatter_dimension=0,
            tiled=True,
        ).astype(jnp.float32),
    )
    key_b = key_local.astype(jnp.bfloat16)
    value_b = value_local.astype(jnp.bfloat16)
    query_b = query_grad.reshape(tok_rows, kv_heads * groups * HD).astype(jnp.bfloat16)
    input_term = jnp.einsum("tk,dk->td", query_b, w_query, preferred_element_type=jnp.float32)
    input_term = input_term + jnp.einsum(
        "tk,dk->td", key_b, w_key, preferred_element_type=jnp.float32
    )
    input_term = input_term + jnp.einsum(
        "tk,dk->td", value_b, w_value, preferred_element_type=jnp.float32
    )
    grad_x = lax.psum_scatter(
        input_term.astype(jnp.bfloat16), "tp", scatter_dimension=1, tiled=True
    )
    grads_cat = jnp.concatenate([query_b, key_b, value_b], axis=1)
    weight_partial = jnp.einsum(
        "td,tk->dk",
        lax.all_gather(layer_input, "tp", axis=1, tiled=True),
        grads_cat,
        preferred_element_type=jnp.float32,
    )
    weight_sum = lax.psum_scatter(
        weight_partial.astype(jnp.bfloat16), "ctx", scatter_dimension=0, tiled=True
    ).astype(jnp.float32)
    query_cols = query_b.shape[1]
    key_cols = key_b.shape[1]
    grad_w_query = weight_sum[:, :query_cols].astype(jnp.bfloat16)
    grad_w_key = weight_sum[:, query_cols : query_cols + key_cols].astype(jnp.bfloat16)
    grad_w_value = weight_sum[:, query_cols + key_cols :].astype(jnp.bfloat16)
    return (grad_x, grad_w_query, grad_w_key, grad_w_value)


def solution(mesh):
    return jax.shard_map(
        shards,
        mesh=mesh,
        in_specs=(
            P("ctx", "tp"),
            P(None, "tp"),
            P(None, "tp"),
            P(None, "tp"),
            P("ctx", "tp"),
            P("ctx", "tp"),
            P("ctx", "tp"),
            P("ctx", "tp"),
            P("ctx", None),
            P(),
        ),
        out_specs=(P("ctx", "tp"), P("ctx", "tp"), P("ctx", "tp"), P("ctx", "tp")),
        check_vma=False,
    )
```

profile of v0, /device:TPU:0, one launch (start us, length us, event | category | flops | bytes accessed | tf_op | source)
XLA Modules:
  0.0 666.4 jit_solution(14086286960479362764)
XLA Ops:
  45.6 4.3 copy.191
  53.7 12.3 %fusion.57 = (f32[4,2,5,128]{3,2,1,0:T(8,128)S(1)}, f32[4,2,8,128,128,5]{4,3,5,2,1,0:T(8,128)}) fusion(pred[4,128,8,128]{1,3,2,0:T(8,128)(4,1)S(1)} %or_and_fusion, bf16[4,128,2,5,128,1]{4,1,3,5,2,0:T(8,128)(2,1)} %copy.250, bf16[4,8,128,2,128,1]{4,2,3,1,0,5:T(8,128)(2,1)} %bitcast.253), kind=kOutput, calls=%fused_computation.86 | convolution fusion | flops 1357900800 | bytes 24924160 | tf_op jit(solution)/shard_map/ithgd,isuhd->ihgtsu/dot_general | solution.py:20
  66.0 10.9 %select_reduce_fusion = f32[4,2,5,128]{3,2,1,0:T(8,128)S(1)} fusion(f32[4,2,8,128,128,5]{4,3,5,2,1,0:T(8,128)} %get-tuple-element.213, f32[4,2,5,128]{3,2,1,0:T(8,128)S(1)} %get-tuple-element.212, pred[4,128,8,128]{1,3,2,0:T(8,128)(4,1)S(1)} %or_and_fusion), kind=kLoop, calls=%fused_computation.82 | loop fusion | flops 26209280 | bytes 21536768 | tf_op jit(solution)/shard_map/reduce_sum | solution.py:25
  79.2 7.4 %fusion.55 = bf16[4,2,5,128,8,128]{3,5,2,4,1,0:T(8,128)(2,1)} fusion(f32[4,2,8,128,128,5]{4,3,5,2,1,0:T(8,128)S(1)} %copy-done.1, f32[4,2,5,128]{3,2,1,0:T(8,128)S(1)} %log_add_fusion.2, pred[4,128,8,128]{1,3,2,0:T(8,128)(4,1)S(1)} %or_and_fusion), kind=kLoop, calls=%fused_computation.84 | loop fusion | flops 26214400 | bytes 32002048 | tf_op jit(solution)/shard_map/convert_element_type | solution.py:29
  86.6 4.3 reshape.553
  98.1 6.8 %fusion.62 = f32[4,128,2,5]{1,3,2,0:T(8,128)S(1)} fusion(bf16[4,128,2,5,128]{1,0,4,3,2:T(4,128)(2,1)} %reshape.484, bf16[4,2,5,128,8,128]{3,5,2,4,1,0:T(8,128)(2,1)} %fusion.55, bf16[4,8,128,2,128,1]{4,2,3,1,0,5:T(8,128)(2,1)} %bitcast.261), kind=kOutput, calls=%fused_computation.93 | convolution fusion | flops 1344138240 | bytes 13914112 | tf_op jit(solution)/shard_map/ihgtsu,isuhd->ithgd/dot_general | solution.py:30
  104.8 15.0 %fusion.54 = bf16[4,2,5,128,8,128]{3,5,2,4,1,0:T(8,128)(2,1)} fusion(f32[4,2,8,128,128,5]{4,3,5,2,1,0:T(8,128)} %get-tuple-element.213, f32[4,2,5,128]{3,2,1,0:T(8,128)S(1)} %bitcast.267, f32[4,2,5,128]{3,2,1,0:T(8,128)S(1)} %log_add_fusion.2, pred[4,128,8,128]{1,3,2,0:T(8,128)(4,1)S(1)} %or_and_fusion, bf16[4,128,2,5,128,1]{4,1,3,5,2,0:T(8,128)(2,1)} %copy.252, ...), kind=kOutput, calls=%fused_computation.79 | convolution fusion | flops 1384120320 | bytes 35430400 | tf_op jit(solution)/shard_map/ithgd,isuhd->ihgtsu/dot_general | solution.py:35
  119.8 5.8 convolution_bitcast_fusion.9
  130.5 9.7 %scatter_fusion = f32[32,128,2,128]{3,1,2,0:T(8,128)} fusion(f32[32,128,2,128]{3,1,2,0:T(8,128)} %broadcast.298.clone, s32[32]{0:T(128)S(1)} %fusion.82, f32[32,128,2,128]{3,1,2,0:T(8,128)} %bitcast.250), kind=kCustom, calls=%fused_computation.2 | custom fusion | flops 1048576 | bytes 12583040 | tf_op jit(solution)/shard_map/scatter-add | solution.py:132
  154.5 11.1 %conditional.2 = (f32[128,2,5,128]{3,0,2,1:T(8,128)S(1)}, f32[2048,2,128]{2,0,1:T(8,128)}, f32[2048,2,128]{2,0,1:T(8,128)}) conditional(s32[]{:T(128)} %convert_element_type.71, () %tuple.40, (s32[2048]{0:T(1024)S(1)}, s32[]{:T(128)}, s32[128,1]{0,1:T(1,128)S(1)}, s32[]{:T(128)}, bf16[512,2,5,128]{0,3,2,1:T(8,128)(2,1)}, ...), branch_computations={%region_4.5_spmd, %region_5.9_spmd} | conditional | flops 4095440384 | bytes 145240736 | solution.py:176
  165.6 8.9 %conditional.3 = (f32[128,2,5,128]{3,0,2,1:T(8,128)}, f32[2048,2,128]{2,0,1:T(8,128)}, f32[2048,2,128]{2,0,1:T(8,128)}) conditional(s32[]{:T(128)} %convert_element_type.72, () %tuple.42, (s32[2048]{0:T(1024)S(1)}, s32[]{:T(128)}, s32[128,1]{0,1:T(1,128)S(1)}, s32[]{:T(128)}, bf16[512,2,5,128]{0,3,2,1:T(8,128)(2,1)}, ...), branch_computations={%region_9.10_spmd, %region_10.14_spmd} | conditional | flops 4095440384 | bytes 145240736 | solution.py:176
  185.0 6.0 convolution_bitcast_fusion.8
  196.0 9.7 %scatter_fusion.1 = f32[32,128,2,128]{3,1,2,0:T(8,128)} fusion(f32[32,128,2,128]{3,1,2,0:T(8,128)} %broadcast.298.clone.1, s32[32]{0:T(128)S(1)} %copy-done.17, f32[32,128,2,128]{3,1,2,0:T(8,128)} %bitcast.249), kind=kCustom, calls=%fused_computation.3 | custom fusion | flops 1048576 | bytes 12583040 | tf_op jit(solution)/shard_map/scatter-add | solution.py:137
  220.8 7.9 %fusion.73 = f32[4,128,2,5,128]{4,1,3,2,0:T(8,128)S(1)} fusion(bf16[4,2,5,128,8,128]{3,5,2,4,1,0:T(8,128)(2,1)} %fusion.54, bf16[4,8,128,2,128,1]{4,2,3,1,0,5:T(8,128)(2,1)} %bitcast.254), kind=kOutput, calls=%fused_computation.111 | convolution fusion | flops 1342177280 | bytes 15204352 | tf_op jit(solution)/shard_map/ihgtsu,isuhd->ithgd/dot_general | solution.py:39
  233.9 73.2 %reduce-scatter.7.cloned.1.call-done = bf16[512,256]{0,1:T(8,128)(2,1)} async-done(((bf16[4096,256]{0,1:T(8,128)(2,1)}), bf16[512,256]{0,1:T(8,128)(2,1)}) %reduce-scatter.7.cloned.1.call-update) | async-done | bytes 262160 | tf_op jit(solution)/shard_map/reduce_scatter | solution.py:182
  307.1 44.8 %reduce-scatter.9.cloned.1.call-done = bf16[512,256]{0,1:T(8,128)(2,1)} async-done(((bf16[4096,256]{0,1:T(8,128)(2,1)}), bf16[512,256]{0,1:T(8,128)(2,1)}) %reduce-scatter.9.cloned.1.call-update) | async-done | bytes 262160 | tf_op jit(solution)/shard_map/reduce_scatter | solution.py:188
  351.9 49.1 %all-gather.8.cloned.1.call-done = bf16[512,5120]{1,0:T(8,128)(2,1)} async-done(((bf16[512,1280]{1,0:T(8,128)(2,1)}), bf16[512,5120]{1,0:T(8,128)(2,1)}) %all-gather.8.cloned.1.call-update) | async-done | bytes 5242896 | tf_op jit(solution)/shard_map/all_gather | solution.py:211
  401.0 15.8 %fusion.56 = bf16[5120,1792]{0,1:T(8,128)(2,1)} fusion(bf16[512,5120]{1,0:T(8,128)(2,1)} %all-gather.8.cloned.1.call-done, bf16[512,256]{0,1:T(8,128)(2,1)} %reduce-scatter.9.cloned.1.call-done, bf16[512,256]{0,1:T(8,128)(2,1)} %reduce-scatter.7.cloned.1.call-done, bf16[512,1280]{0,1:T(8,128)(2,1)} %bitcast.263), kind=kOutput, calls=%fused_computation.85 | convolution fusion | flops 9409921024 | bytes 25427968 | tf_op jit(solution)/shard_map/td,tk->dk/dot_general | solution.py:209
  416.8 23.2 %copy.291 = bf16[5120,1792]{1,0:T(8,128)(2,1)} copy(bf16[5120,1792]{0,1:T(8,128)(2,1)} %fusion.56) | data formatting | bytes 36700160
  440.3 15.9 %fusion.87 = f32[512,5120]{1,0:T(8,128)} fusion(bf16[512,1280]{0,1:T(8,128)(2,1)} %bitcast.264, bf16[5120,1280]{1,0:T(8,128)(2,1)} %param.23), kind=kOutput, calls=%fused_computation.134 | convolution fusion | flops 6710886400 | bytes 24903680 | tf_op jit(solution)/shard_map/tk,dk->td/dot_general | solution.py:198
  456.2 7.4 %fusion.88 = f32[512,5120]{1,0:T(8,128)} fusion(bf16[512,256]{0,1:T(8,128)(2,1)S(1)} %copy-done.14, bf16[5120,256]{1,0:T(8,128)(2,1)S(1)} %copy-done), kind=kOutput, calls=%fused_computation.135 | convolution fusion | flops 1342177280 | bytes 13369344 | tf_op jit(solution)/shard_map/tk,dk->td/dot_general | solution.py:199
  463.7 12.3 %add_convert_fusion = bf16[512,5120]{1,0:T(8,128)(2,1)} fusion(f32[512,5120]{1,0:T(8,128)} %fusion.87, f32[512,5120]{1,0:T(8,128)} %fusion.88, bf16[512,256]{0,1:T(8,128)(2,1)S(1)} %copy-done.13, bf16[5120,256]{1,0:T(8,128)(2,1)S(1)} %copy-done.10), kind=kOutput, calls=%fused_computation.91 | convolution fusion | flops 1350041600 | bytes 29097984 | tf_op jit(solution)/shard_map/tk,dk->td/dot_general | solution.py:202
  476.0 85.8 %reduce-scatter.13.cloned.1.call-done = bf16[640,1792]{1,0:T(8,128)(2,1)} async-done(((bf16[5120,1792]{1,0:T(8,128)(2,1)}), bf16[640,1792]{1,0:T(8,128)(2,1)}) %reduce-scatter.13.cloned.1.call-update) | async-done | bytes 2293776
  566.4 92.0 %reduce-scatter.11.cloned.1.call-done = bf16[512,1280]{1,0:T(8,128)(2,1)} async-done(((bf16[512,5120]{1,0:T(8,128)(2,1)}), bf16[512,1280]{1,0:T(8,128)(2,1)}) %reduce-scatter.11.cloned.1.call-update) | async-done | bytes 1310736 | tf_op jit(solution)/shard_map/reduce_scatter | solution.py:205
  (105 shorter events, 113.7 us)
Async XLA Ops:
  8.0 448.2 %copy-start = (bf16[5120,256]{1,0:T(8,128)(2,1)S(1)}, bf16[5120,256]{1,0:T(8,128)(2,1)}, u32[]{:S(2)}) copy-start(bf16[5120,256]{1,0:T(8,128)(2,1)} %param.24) | copy-start | bytes 7864324
  8.0 19.7 %copy-start.15 = (s32[2]{0:T(128)S(1)}, s32[2]{0:T(128)}, u32[]{:S(2)}) copy-start(s32[2]{0:T(128)} %param.31) | copy-start | bytes 28
  8.0 34.2 %all-gather.4.cloned.1.call-start = ((), (), s32[]{:S(2)}) async-start(), calls=%async_computation.4 | async-start | bytes 2359296 | tf_op jit(solution)/shard_map/all_gather | solution.py:102
  10.0 76.6 %all-gather.6.cloned.1.call-start = ((), (), s32[]{:S(2)}) async-start(), calls=%async_computation.5 | async-start | bytes 2359296 | tf_op jit(solution)/shard_map/all_gather | solution.py:103
  10.8 296.4 %reduce-scatter.7.cloned.1.call-start = ((), (), s32[]{:S(2)}) async-start(), calls=%async_computation.6 | async-start | bytes 2359296 | tf_op jit(solution)/shard_map/reduce_scatter | solution.py:182
  37.5 93.0 %copy-start.16 = (s32[32]{0:T(128)}, s32[32]{0:T(128)S(1)}, u32[]{:S(2)}) copy-start(s32[32]{0:T(128)S(1)} %fusion.82) | copy-start | bytes 388
  66.0 13.2 %copy-start.1 = (f32[4,2,8,128,128,5]{4,3,5,2,1,0:T(8,128)S(1)}, f32[4,2,8,128,128,5]{4,3,5,2,1,0:T(8,128)}, u32[]{:S(2)}) copy-start(f32[4,2,8,128,128,5]{4,3,5,2,1,0:T(8,128)} %get-tuple-element.213) | copy-start | bytes 62914564
  104.8 15.0 %copy-start.8 = (bf16[4,128,2,5,128,1]{4,1,3,5,2,0:T(8,128)(2,1)S(1)}, bf16[4,128,2,5,128,1]{4,1,3,5,2,0:T(8,128)(2,1)}, u32[]{:S(2)}) copy-start(bf16[4,128,2,5,128,1]{4,1,3,5,2,0:T(8,128)(2,1)} %copy.250) | copy-start | bytes 3932164
  140.2 4.0 copy-start.3
  140.2 5.5 copy-start.9
  185.0 166.9 %reduce-scatter.9.cloned.1.call-start = ((), (), s32[]{:S(2)}) async-start(), calls=%async_computation.7 | async-start | bytes 2359296 | tf_op jit(solution)/shard_map/reduce_scatter | solution.py:188
  191.1 4.9 copy-start.17
  205.7 4.0 copy-start.2
  219.9 181.1 %all-gather.8.cloned.1.call-start = ((), (), s32[]{:S(2)}) async-start(), calls=%async_computation.9 | async-start | bytes 6553600 | tf_op jit(solution)/shard_map/all_gather | solution.py:211
  220.5 341.3 %reduce-scatter.13.cloned.1.call-start = ((), (), s32[]{:S(2)}) async-start(), calls=%async_computation.10 | async-start | bytes 20643840
  440.0 16.2 %copy-start.14 = (bf16[512,256]{0,1:T(8,128)(2,1)S(1)}, bf16[512,256]{0,1:T(8,128)(2,1)}, u32[]{:S(2)}) copy-start(bf16[512,256]{0,1:T(8,128)(2,1)} %reduce-scatter.7.cloned.1.call-done) | copy-start | bytes 786436
  440.0 218.4 %reduce-scatter.11.cloned.1.call-start = ((), (), s32[]{:S(2)}) async-start(), calls=%async_computation.8 | async-start | bytes 6553600 | tf_op jit(solution)/shard_map/reduce_scatter | solution.py:205
  456.2 7.4 %copy-start.10 = (bf16[5120,256]{1,0:T(8,128)(2,1)S(1)}, bf16[5120,256]{1,0:T(8,128)(2,1)}, u32[]{:S(2)}) copy-start(bf16[5120,256]{1,0:T(8,128)(2,1)} %param.25) | copy-start | bytes 7864324
  456.2 7.4 %copy-start.13 = (bf16[512,256]{0,1:T(8,128)(2,1)S(1)}, bf16[512,256]{0,1:T(8,128)(2,1)}, u32[]{:S(2)}) copy-start(bf16[512,256]{0,1:T(8,128)(2,1)} %reduce-scatter.9.cloned.1.call-done) | copy-start | bytes 786436
Sparse Core Ops, SparseCore 0:
  11.3 30.8 all-gather.3
  44.1 27.9 all-gather.5
  185.1 122.0 reduce-scatter.6
  310.6 41.2 reduce-scatter.8
  440.1 121.6 reduce-scatter.12
  564.6 93.7 reduce-scatter.10
Sparse Core Ops, SparseCore 1:
  222.0 179.0 all-gather.7
where the time goes:
time: 656 us; the launch traced here: 666 us
  waiting for transfers between devices  350 us (53%)
  local copies, waits for them, and re-layouts  122 us (19%)
  matrix products  105 us (16%)
  other arithmetic  55.1 us (8%)
  between operations  20.1 us (3%)
  loops' own time  13.2 us (2%)
    reduce_scatter x1, waiting for transfers between devices, shards(): lax.psum_scatter(input_term.astype(jnp.bfloat16), 'tp', scatter_dimension...  92 us
    unnamed x8, waiting for transfers between devices  87.1 us
    reduce_scatter x1, waiting for transfers between devices, shards(): lax.psum_scatter(key_grad_all.reshape(total_rows, key_cols_all).astype(jn...  73.2 us
    all_gather x1, waiting for transfers between devices, shards(): lax.all_gather(layer_input, 'tp', axis=1, tiled=True)  49.1 us
    reduce_scatter x1, waiting for transfers between devices, shards(): lax.psum_scatter(value_grad_all.reshape(total_rows, key_cols_all).astype(...  44.8 us
    unnamed x29, local copies, waits for them, and re-layouts  35.7 us
    another operation x12, local copies, waits for them, and re-layouts  16.6 us
    dot_general x1, matrix products, shards(): jnp.einsum('tk,dk->td', query_b, w_query, preferred_element_type=jnp.floa...  15.9 us
  transfers between devices with their start and end apart: 7, of which 6 were waited for; matrix products, arithmetic and copies ran while one was open for 23% of the time, Pallas kernels for 0%

commit v1 on v0

v1 whole, which is shorter than its diff:
```python
import functools
import math

import jax
import jax.numpy as jnp
from jax import lax
from jax.experimental import pallas as pl
from jax.experimental.pallas import tpu as pltpu
from jax.sharding import PartitionSpec as P

H = 40
KVH = 8
HD = 128
BLK = 128
NGLOB = 2
GROUPS = H // KVH
ROWS = GROUPS * BLK
SCALE = 1.0 / math.sqrt(HD)
EXP_SCALE = SCALE * math.log2(math.e)
MASKED = -1e30
BF16 = jnp.bfloat16
F32 = jnp.float32
MIB = 1024 * 1024


def fold_rows(x):
    return x.reshape(x.shape[0] // 8, 8, x.shape[1])


def attn_kernel(places, tok_rows, lists, globs, here, q_ref, do_ref, *refs):
    pieces, refs = refs[: len(places)], refs[len(places) :]
    dq_ref, same_ref, other_ref, kv_ref, s_ref, dp_ref, dqt_ref, dk_acc, dv_acc, ids = refs
    step = pl.program_id(0)
    me = here[0]
    ctx_size = kv_ref.shape[0] // tok_rows

    @pl.when(step == 0)
    def _():
        dk_acc[...] = jnp.zeros_like(dk_acc)
        dv_acc[...] = jnp.zeros_like(dv_acc)
        for (mask, offset), piece in zip(places, pieces):
            start = pl.multiple_of((me ^ mask) * tok_rows + offset, BLK)
            kv_ref[pl.ds(start, piece.shape[0]), :] = piece[...]

    blk = me * (tok_rows // BLK) + step
    is_global = globs[0] == blk
    for g in range(1, NGLOB):
        is_global = is_global | (globs[g] == blk)

    def all_before():
        def put(i, carry):
            ids[2 + i] = i
            return carry

        lax.fori_loop(0, blk, put, 0)
        return blk

    def listed():
        count = jnp.int32(0)
        for slot in range(lists.shape[1]):
            other = lists[step, slot]
            ids[2 + count] = jnp.maximum(other, 0)
            count = count + jnp.where((other >= 0) & (other != blk), 1, 0)
        for g in range(NGLOB):
            other = globs[g]
            ids[2 + count] = other
            count = count + jnp.where(other <= blk, 1, 0)
        return count

    count = lax.cond(is_global, all_before, listed)
    odd = lax.rem(count, 2) == 1
    last = ids[1 + count]
    ids[0] = blk
    ids[1] = jnp.where(odd, last, blk)
    pairs = 1 + lax.div(count, 2)

    def stacked(ref):
        return jnp.concatenate([ref[:, g * HD : (g + 1) * HD] for g in range(GROUPS)], axis=0)

    q_rows = stacked(q_ref)
    do_rows = stacked(do_ref)
    q_cols = q_rows.T
    do_cols = do_rows.T

    def start_of(i):
        return pl.multiple_of(ids[i] * BLK, BLK)

    def pair_rows(p, half):
        cols = slice(half * HD, (half + 1) * HD)
        return jnp.concatenate(
            [kv_ref[pl.ds(start_of(2 * p), BLK), cols], kv_ref[pl.ds(start_of(2 * p + 1), BLK), cols]],
            axis=0,
        )

    def at(p):
        return pl.ds(pl.multiple_of(p * 2 * BLK, 2 * BLK), 2 * BLK)

    def scores_of(p):
        return jnp.dot(pair_rows(p, 0), q_cols, preferred_element_type=F32)

    key_pos = lax.broadcasted_iota(jnp.int32, (2 * BLK, ROWS), 0)
    query_pos = lax.broadcasted_iota(jnp.int32, (2 * BLK, ROWS), 1) & (BLK - 1)
    limit = jnp.where(odd, 2 * BLK, 0)
    keep = key_pos <= jnp.where(key_pos < BLK, query_pos, limit - 1)
    scores = jnp.where(keep, scores_of(0), MASKED)
    s_ref[at(0), :] = scores
    top8 = jnp.max(fold_rows(scores), axis=0)

    def score_pass(p, top8):
        scores = scores_of(p)
        s_ref[at(p), :] = scores
        return jnp.maximum(top8, jnp.max(fold_rows(scores), axis=0))

    top8 = lax.fori_loop(1, pairs, score_pass, top8)
    top = jnp.max(top8, axis=0, keepdims=True)

    def sum_pass(p, carry):
        total8, dot8 = carry
        e = jnp.exp2((s_ref[at(p), :] - top) * EXP_SCALE)
        dp = jnp.dot(pair_rows(p, 1), do_cols, preferred_element_type=F32)
        s_ref[at(p), :] = e
        dp_ref[at(p), :] = dp
        return (
            total8 + jnp.sum(fold_rows(e), axis=0),
            dot8 + jnp.sum(fold_rows(e * dp), axis=0),
        )

    zero8 = jnp.zeros((8, ROWS), F32)
    total8, dot8 = lax.fori_loop(0, pairs, sum_pass, (zero8, zero8))
    inverse = 1.0 / jnp.sum(total8, axis=0, keepdims=True)
    delta = jnp.sum(dot8, axis=0, keepdims=True) * inverse
    dqt_ref[...] = jnp.zeros_like(dqt_ref)

    def grad_pass(p, carry):
        prob = s_ref[at(p), :] * inverse
        ds = (prob * (dp_ref[at(p), :] - delta)).astype(BF16)
        dv = jnp.dot(prob.astype(BF16), do_rows, preferred_element_type=F32)
        dk = jnp.dot(ds, q_rows, preferred_element_type=F32)
        dqt_ref[...] += jnp.dot(pair_rows(p, 0).T, ds, preferred_element_type=F32)
        for half in range(2):
            rows = pl.ds(start_of(2 * p + half), BLK)
            part = slice(half * BLK, (half + 1) * BLK)
            dk_acc[rows, :] += dk[part]
            dv_acc[rows, :] += dv[part]
        return carry

    lax.fori_loop(0, pairs, grad_pass, 0)
    dq = (dqt_ref[...] * SCALE).T.astype(BF16)
    for g in range(GROUPS):
        dq_ref[:, g * HD : (g + 1) * HD] = dq[g * BLK : (g + 1) * BLK]

    @pl.when(step == pl.num_programs(0) - 1)
    def _():
        for chip in range(ctx_size // 2):
            out = slice(chip * tok_rows, (chip + 1) * tok_rows)
            for ref, core in ((same_ref, 0), (other_ref, 1)):
                start = pl.multiple_of((me ^ (2 * chip + core)) * tok_rows, BLK)
                rows = pl.ds(start, tok_rows)
                ref[out, :HD] = (dk_acc[rows, :] * SCALE).astype(BF16)
                ref[out, HD:] = dv_acc[rows, :].astype(BF16)


def attention_grads(head, block_lists, global_ids, here, queries, grad_out, places, pieces):
    tok_rows = queries.shape[0]
    blk_count = tok_rows // BLK
    total_rows = sum(piece.shape[0] for piece in pieces)
    slots = max(block_lists.shape[1] + NGLOB + 2, total_rows // BLK // 2 + 2)
    slots += slots % 2
    smem = pl.BlockSpec(memory_space=pltpu.SMEM)
    pair_cols = 2 * HD
    work = blk_count * 9 * BLK * ROWS
    half = pl.BlockSpec((total_rows // 2, pair_cols), lambda a: (0, 0))
    half_shape = jax.ShapeDtypeStruct((total_rows // 2, pair_cols), BF16)
    return pl.pallas_call(
        functools.partial(attn_kernel, places, tok_rows),
        grid=(blk_count,),
        in_specs=[
            smem,
            smem,
            smem,
            pl.BlockSpec((BLK, ROWS), lambda a: (a, head)),
            pl.BlockSpec((BLK, ROWS), lambda a: (a, head)),
        ]
        + [
            pl.BlockSpec(
                (piece.shape[0], pair_cols), lambda a: (0, head), pipeline_mode=pl.Buffered(1)
            )
            for piece in pieces
        ],
        out_specs=[pl.BlockSpec((BLK, ROWS), lambda a: (a, 0)), half, half],
        out_shape=[jax.ShapeDtypeStruct((tok_rows, ROWS), BF16), half_shape, half_shape],
        scratch_shapes=[
            pltpu.VMEM((total_rows, pair_cols), BF16),
            pltpu.VMEM((slots * BLK, ROWS), F32),
            pltpu.VMEM((slots * BLK, ROWS), F32),
            pltpu.VMEM((HD, ROWS), F32),
            pltpu.VMEM((total_rows, HD), F32),
            pltpu.VMEM((total_rows, HD), F32),
            pltpu.SMEM((slots + 4,), jnp.int32),
        ],
        compiler_params=pltpu.CompilerParams(
            dimension_semantics=("arbitrary",), vmem_limit_bytes=58 * MIB
        ),
        cost_estimate=pl.CostEstimate(
            flops=10 * work * HD,
            transcendentals=work,
            bytes_accessed=4 * total_rows * pair_cols + 6 * tok_rows * ROWS,
        ),
        name="attn_grads",
    )(block_lists, global_ids, here, queries, grad_out, *pieces)


def input_grad_kernel(heads, *refs):
    dq, dkv = refs[:heads], refs[heads : 2 * heads]
    wq_ref, wk_ref, wv_ref, out_ref, dk_ref, dv_ref = refs[2 * heads :]

    @pl.when(pl.program_id(0) == 0)
    def _():
        for j in range(heads):
            cols = slice(j * HD, (j + 1) * HD)
            dk_ref[:, cols] = dkv[j][:, :HD]
            dv_ref[:, cols] = dkv[j][:, HD:]

    def term(grad, weight):
        return lax.dot_general(
            grad, weight, (((1,), (1,)), ((), ())), preferred_element_type=F32
        )

    total = term(dk_ref[...], wk_ref[...]) + term(dv_ref[...], wv_ref[...])
    for j in range(heads):
        total += term(dq[j][...], wq_ref[:, j * ROWS : (j + 1) * ROWS])
    out_ref[...] = total.astype(BF16)


def input_grad(dq, dkv, w_query, w_key, w_value):
    heads = len(dq)
    rows, width = dq[0].shape[0], w_query.shape[0]
    tile = 512
    whole = [pl.BlockSpec(x.shape, lambda i: (0, 0)) for x in dq + dkv]
    cols = w_query.shape[1] + w_key.shape[1] + w_value.shape[1]
    return pl.pallas_call(
        functools.partial(input_grad_kernel, heads),
        grid=(width // tile,),
        in_specs=whole
        + [pl.BlockSpec((tile, w.shape[1]), lambda i: (i, 0)) for w in (w_query, w_key, w_value)],
        out_specs=pl.BlockSpec((rows, tile), lambda i: (0, i)),
        out_shape=jax.ShapeDtypeStruct((rows, width), BF16),
        scratch_shapes=[pltpu.VMEM((rows, heads * HD), BF16)] * 2,
        compiler_params=pltpu.CompilerParams(
            dimension_semantics=("arbitrary",), vmem_limit_bytes=40 * MIB
        ),
        cost_estimate=pl.CostEstimate(
            flops=2 * rows * width * cols,
            transcendentals=0,
            bytes_accessed=2 * (width * cols + rows * cols + rows * width),
        ),
        name="input_grad",
    )(*dq, *dkv, w_query, w_key, w_value)


def weight_grad_kernel(count, chip, x_ref, *refs):
    out_ref = refs[-1]
    own, partner = refs[:count], refs[count : 2 * count]
    inputs = x_ref[0].T
    rows = own[0].shape[0]
    start = 0
    for mine, theirs in zip(own, partner):
        total = jnp.dot(inputs[:, :rows], mine[...], preferred_element_type=F32)
        total += jnp.dot(inputs[:, rows:], theirs[...], preferred_element_type=F32)
        cols = mine.shape[1]
        out_ref[0, :, start : start + cols] = total.astype(BF16)
        start += cols


def weight_grad(chip, inputs, own, partner):
    chips, rows, width = inputs.shape
    cols = sum(x.shape[1] for x in own)
    return pl.pallas_call(
        functools.partial(weight_grad_kernel, len(own)),
        grid_spec=pltpu.PrefetchScalarGridSpec(
            num_scalar_prefetch=1,
            grid=(chips,),
            in_specs=[pl.BlockSpec((1, rows, width), lambda i, chip: (chip[0] ^ i, 0, 0))]
            + [pl.BlockSpec(x.shape, lambda i, chip: (0, 0)) for x in own + partner],
            out_specs=pl.BlockSpec((1, width, cols), lambda i, chip: (i, 0, 0)),
        ),
        out_shape=jax.ShapeDtypeStruct((chips, width, cols), BF16),
        compiler_params=pltpu.CompilerParams(
            dimension_semantics=("arbitrary",), vmem_limit_bytes=40 * MIB
        ),
        cost_estimate=pl.CostEstimate(
            flops=2 * chips * rows * width * cols,
            transcendentals=0,
            bytes_accessed=2 * (chips * width * (rows + cols) + rows * cols),
        ),
        name="weight_grad",
    )(chip, inputs, *own, *partner)


def swap(x, mask):
    return lax.ppermute(x, "ctx", [(i, i ^ mask) for i in range(lax.axis_size("ctx"))])


def gather_pieces(x):
    rows = x.shape[0]
    chips = lax.axis_size("ctx") // 2
    found = [((0, 0), x)]
    if chips == 4:
        side, front = swap(x, 2), swap(x, 4)
        half = rows // 2
        found += [((2, 0), side), ((4, 0), front)]
        found += [((6, 0), swap(front[:half], 2)), ((6, half), swap(side[half:], 4))]
    else:
        found += [((2 * i, 0), swap(x, 2 * i)) for i in range(1, chips)]
    found += [((mask ^ 1, offset), swap(piece, 1)) for (mask, offset), piece in found]
    return [place for place, _ in found], [piece for _, piece in found]


def total_of(parts):
    total = parts[0].astype(F32)
    for part in parts[1:]:
        total = total + part.astype(F32)
    return total.astype(BF16)


def shards(
    layer_input, w_query, w_key, w_value, queries, keys, values, grad_out, block_lists, global_ids
):
    tok_rows, width = layer_input.shape
    kv_heads = keys.shape[1] // HD
    chips = lax.axis_size("ctx") // 2
    here = lax.axis_index("ctx").astype(jnp.int32)
    core = here % 2
    chip = (here // 2).reshape(1)

    kv_own = jnp.concatenate(
        [
            x[:, j * HD : (j + 1) * HD]
            for j in range(kv_heads)
            for x in (keys, values)
        ],
        axis=1,
    )
    places, pieces = gather_pieces(kv_own)

    half = width // 2
    kept = lax.dynamic_slice_in_dim(layer_input, core * half, half, 1)
    given = lax.dynamic_slice_in_dim(layer_input, (1 - core) * half, half, 1)
    input_pair = jnp.concatenate([kept, swap(given, 1)], axis=0)
    runs = 2
    step = half // runs
    inputs = [
        lax.all_gather(input_pair[:, r * step : (r + 1) * step], "tp", axis=0, tiled=False)
        for r in range(runs)
    ]

    dq, dkv = [], []
    for j in range(kv_heads):
        dq_j, same, other = attention_grads(
            j, block_lists, global_ids, here.reshape(1), queries, grad_out, places, pieces
        )
        dq.append(dq_j)
        chip_sum = total_of([same, swap(other, 1)]).reshape(chips, tok_rows, 2 * HD)
        dkv.append(total_of([chip_sum[0]] + [swap(chip_sum[i], 2 * i) for i in range(1, chips)]))
    dq_partner = [swap(x, 1) for x in dq]
    dkv_partner = [swap(x, 1) for x in dkv]

    grad_x = lax.psum_scatter(
        input_grad(dq, dkv, w_query, w_key, w_value), "tp", scatter_dimension=1, tiled=True
    )

    def scattered(partial):
        return total_of([partial[0]] + [swap(partial[i], 2 * i) for i in range(1, chips)])

    grad_w_query = jnp.concatenate(
        [scattered(weight_grad(chip, x, dq, dq_partner)) for x in inputs], axis=0
    )
    grad_w_kv = jnp.concatenate(
        [scattered(weight_grad(chip, x, dkv, dkv_partner)) for x in inputs], axis=0
    )

    def columns(first):
        return jnp.concatenate(
            [grad_w_kv[:, c : c + HD] for c in range(first, 2 * HD * kv_heads, 2 * HD)], axis=1
        )

    return (grad_x, grad_w_query, columns(0), columns(HD))


def solution(mesh):
    return jax.shard_map(
        shards,
        mesh=mesh,
        in_specs=(
            P("ctx", "tp"),
            P(None, "tp"),
            P(None, "tp"),
            P(None, "tp"),
            P("ctx", "tp"),
            P("ctx", "tp"),
            P("ctx", "tp"),
            P("ctx", "tp"),
            P("ctx", None),
            P(),
        ),
        out_specs=(P("ctx", "tp"), P("ctx", "tp"), P("ctx", "tp"), P("ctx", "tp")),
        check_vma=False,
    )
```

time: 656 us -> 254 us (0.39); the launches traced: 666 us -> 253 us
  waiting for transfers between devices: 350 us -> 112 us
  local copies, waits for them, and re-layouts: 122 us -> 11.9 us
  matrix products: 105 us -> 0 us
  starting transfers between devices: 0.83 us -> 54.2 us
  Pallas kernels: 0 us -> 53.2 us
  other arithmetic: 55.1 us -> 7.63 us
  loops' own time: 13.2 us -> 0 us
    reduce_scatter x3 -> x1, waiting for transfers between devices: 210 us -> 0.01 us  [shards(): lax.psum_scatter(input_grad(dq, dkv, w_query, w_key, w_value), 'tp', scat...]
    ppermute x0 -> x34, waiting for transfers between devices: none -> 110 us  [swap(): lax.ppermute(x, 'ctx', [(i, i ^ mask) for i in range(lax.axis_size('ctx'))])]
    dot_general x10 -> x0, matrix products: 105 us -> none  [the longest x1 15.9 us: shards(): jnp.einsum('tk,dk->td', query_b, w_query, preferred_element_type=jnp.floa...]
    unnamed x8 -> x3, waiting for transfers between devices: 87.1 us -> 0.05 us
    ppermute x0 -> x34, starting transfers between devices: none -> 53.9 us  [swap(): lax.ppermute(x, 'ctx', [(i, i ^ mask) for i in range(lax.axis_size('ctx'))])]
    pallas_call x0 -> x7, Pallas kernels: none -> 53.2 us  [the longest x2 20.7 us: attention_grads(): pl.pallas_call(functools.partial(attn_kernel, places, tok_rows), grid=(bl...]
    all_gather x3 -> x2, waiting for transfers between devices: 53.3 us -> 1.63 us  [shards(): lax.all_gather(input_pair[:, r * step:(r + 1) * step], 'tp', axis=0, tile...]
    scatter-add x6 -> x0, other arithmetic: 31.3 us -> none  [the longest x1 9.68 us: shards(): key_grad_all = jnp.zeros((total_blocks, BLK, kv_heads, HD), jnp.float32)....]
  transfers between devices with their start and end apart: 7 -> 37, of which waited for: 6 -> 19; matrix products, arithmetic and copies ran while one was open for 23% -> 3% of each run, Pallas kernels for 0% -> 21%
where the time goes in v1:
time: 254 us; the launch traced here: 253 us
  waiting for transfers between devices  112 us (44%)
  starting transfers between devices  54.2 us (21%)
  Pallas kernels  53.2 us (21%)
  between operations  14.2 us (6%)
  local copies, waits for them, and re-layouts  11.9 us (5%)
  other arithmetic  7.63 us (3%)
    ppermute x34, waiting for transfers between devices, swap(): lax.ppermute(x, 'ctx', [(i, i ^ mask) for i in range(lax.axis_size('ctx'))])  110 us
    ppermute x34, starting transfers between devices, swap(): lax.ppermute(x, 'ctx', [(i, i ^ mask) for i in range(lax.axis_size('ctx'))])  53.9 us
    pallas_call x2, Pallas kernels, attention_grads(): pl.pallas_call(functools.partial(attn_kernel, places, tok_rows), grid=(bl...  20.7 us
    pallas_call x4, Pallas kernels, weight_grad(): pl.pallas_call(functools.partial(weight_grad_kernel, len(own)), grid_spec...  17.8 us
    pallas_call x1, Pallas kernels, input_grad(): pl.pallas_call(functools.partial(input_grad_kernel, heads), grid=(width /...  14.8 us
    unnamed x44, local copies, waits for them, and re-layouts  8.87 us
  transfers between devices with their start and end apart: 37, of which 19 were waited for; matrix products, arithmetic and copies ran while one was open for 3% of the time, Pallas kernels for 21%

profile of v1, /device:TPU:0, one launch (start us, length us, event | category | flops | bytes accessed | tf_op | source)
XLA Modules:
  0.0 253.1 jit_solution(1089770768257875722)
XLA Ops:
  12.7 3.0 %collective-permute-start.1 = (bf16[512,512]{1,0:T(8,128)(2,1)S(1)}, bf16[512,512]{1,0:T(8,128)(2,1)S(1)}, u32[]{:S(2)}, u32[]{:S(2)}) collective-permute-start(bf16[512,512]{1,0:T(8,128)(2,1)S(1)} %pad_maximum_fusion.2.refs_0_), channel_id=1, source_target_pairs={{0,16},{4,20},{8,24},{12,28},{16,0},{20,4},{24,8},{28,12},{1,17},{... | collective-permute-start | bytes 1572872 | tf_op jit(solution)/shard_map/ppermute | solution.py:301
  17.2 10.7 %collective-permute-done.1.refs_2_ = bf16[512,512]{1,0:T(8,128)(2,1)S(1)} collective-permute-done((bf16[512,512]{1,0:T(8,128)(2,1)S(1)}, bf16[512,512]{1,0:T(8,128)(2,1)S(1)}, u32[]{:S(2)}, u32[]{:S(2)}) %collective-permute-start.1) | collective-permute-done | bytes 524320 | tf_op jit(solution)/shard_map/ppermute | solution.py:301
  31.8 4.1 %collective-permute-done.2.refs_3_ = bf16[256,512]{1,0:T(8,128)(2,1)S(1)} collective-permute-done((bf16[256,512]{1,0:T(8,128)(2,1)S(1)}, bf16[256,512]{1,0:T(8,128)(2,1)S(1)}, u32[]{:S(2)}, u32[]{:S(2)}) %collective-permute-start.2) | collective-permute-done | bytes 262176 | tf_op jit(solution)/shard_map/ppermute | solution.py:301
  39.7 10.3 %attn_grads.3 = (bf16[512,640]{1,0:T(8,128)(2,1)}, bf16[2048,256]{1,0:T(8,128)(2,1)}, bf16[2048,256]{1,0:T(8,128)(2,1)}) custom-call(s32[4,6]{1,0:T(4,128)} %lists.3, s32[2]{0:T(128)} %globs.3, s32[1]{0:T(128)} %bitcast.here, bf16[512,1280]{1,0:T(8,128)(2,1)} %q_ref.3, bf16[512,1280]{1,0:T(8,128)(2,1)} %do_ref.3, bf16[512,512]{1,0:T(8,128)(2,1)} %copy-done.10, ...), custom_call_target="tpu_custom_call" | custom-call | flops 3774873600 | bytes 6160384 | tf_op jit(solution)/shard_map/attn_grads/pallas_call | solution.py:174
  50.1 5.7 %collective-permute-start.13 = (bf16[2048,256]{1,0:T(8,128)(2,1)}, bf16[2048,256]{1,0:T(8,128)(2,1)S(1)}, u32[]{:S(2)}, u32[]{:S(2)}) collective-permute-start(bf16[2048,256]{1,0:T(8,128)(2,1)} %get-tuple-element.15), channel_id=1, source_target_pairs={{0,4},{4,0},{8,12},{12,8},{16,20},{20,16},{24,28},{28,24},{1,5},{5... | collective-permute-start | bytes 3145736 | tf_op jit(solution)/shard_map/ppermute | solution.py:301
  56.0 10.3 %attn_grads.2 = (bf16[512,640]{1,0:T(8,128)(2,1)}, bf16[2048,256]{1,0:T(8,128)(2,1)}, bf16[2048,256]{1,0:T(8,128)(2,1)}) custom-call(s32[4,6]{1,0:T(4,128)} %lists.3, s32[2]{0:T(128)} %globs.3, s32[1]{0:T(128)} %bitcast.here, bf16[512,1280]{1,0:T(8,128)(2,1)} %q_ref.3, bf16[512,1280]{1,0:T(8,128)(2,1)} %do_ref.3, bf16[512,512]{1,0:T(8,128)(2,1)} %copy-done.10, ...), custom_call_target="tpu_custom_call" | custom-call | flops 3774873600 | bytes 6160384 | tf_op jit(solution)/shard_map/attn_grads/pallas_call | solution.py:174
  66.3 5.5 %collective-permute-start.9 = (bf16[2048,256]{1,0:T(8,128)(2,1)}, bf16[2048,256]{1,0:T(8,128)(2,1)S(1)}, u32[]{:S(2)}, u32[]{:S(2)}) collective-permute-start(bf16[2048,256]{1,0:T(8,128)(2,1)} %get-tuple-element.13), channel_id=1, source_target_pairs={{0,4},{4,0},{8,12},{12,8},{16,20},{20,16},{24,28},{28,24},{1,5},{5... | collective-permute-start | bytes 3145736 | tf_op jit(solution)/shard_map/ppermute | solution.py:301
  72.2 15.9 %collective-permute-start.14 = (bf16[512,256]{1,0:T(8,128)(2,1)S(1)}, bf16[512,256]{1,0:T(8,128)(2,1)S(1)}, u32[]{:S(2)}, u32[]{:S(2)}) collective-permute-start(bf16[512,256]{1,0:T(8,128)(2,1)S(1)} %get-tuple-element.32), channel_id=1, source_target_pairs={{0,8},{4,12},{8,0},{12,4},{16,24},{20,28},{24,16},{28,20},{1,9},{5... | collective-permute-start | bytes 786440 | tf_op jit(solution)/shard_map/ppermute | solution.py:301
  90.1 2.0 collective-permute-start.10
  92.1 3.2 %collective-permute-done.14 = bf16[512,256]{1,0:T(8,128)(2,1)S(1)} collective-permute-done((bf16[512,256]{1,0:T(8,128)(2,1)S(1)}, bf16[512,256]{1,0:T(8,128)(2,1)S(1)}, u32[]{:S(2)}, u32[]{:S(2)}) %collective-permute-start.14) | collective-permute-done | bytes 262176 | tf_op jit(solution)/shard_map/ppermute | solution.py:301
  95.3 8.7 %collective-permute-done.15 = bf16[512,256]{1,0:T(8,128)(2,1)S(1)} collective-permute-done((bf16[512,256]{1,0:T(8,128)(2,1)S(1)}, bf16[512,256]{1,0:T(8,128)(2,1)S(1)}, u32[]{:S(2)}, u32[]{:S(2)}) %collective-permute-start.15) | collective-permute-done | bytes 262176 | tf_op jit(solution)/shard_map/ppermute | solution.py:301
  104.1 2.4 collective-permute-done.10
  106.5 6.4 %collective-permute-done.11 = bf16[512,256]{1,0:T(8,128)(2,1)S(1)} collective-permute-done((bf16[512,256]{1,0:T(8,128)(2,1)S(1)}, bf16[512,256]{1,0:T(8,128)(2,1)S(1)}, u32[]{:S(2)}, u32[]{:S(2)}) %collective-permute-start.11) | collective-permute-done | bytes 262176 | tf_op jit(solution)/shard_map/ppermute | solution.py:301
  113.1 14.8 %input_grad.1 = bf16[512,5120]{1,0:T(8,128)(2,1)S(1)} custom-call(bf16[512,640]{1,0:T(8,128)(2,1)} %get-tuple-element.10.refs_0_, bf16[512,640]{1,0:T(8,128)(2,1)S(1)} %copy-done.7, bf16[512,256]{1,0:T(8,128)(2,1)S(1)} %add_convert_fusion.3.refs_2_.refs_0_, bf16[512,256]{1,0:T(8,128)(2,1)S(1)} %add_convert_fusion.2.refs_3_.refs_1_, ...), custom_call_target="tpu_custom_call" | custom-call | flops 9395240960 | bytes 25427968 | tf_op jit(solution)/shard_map/input_grad/pallas_call | solution.py:241
  128.0 2.3 copy-done
  134.2 2.2 weight_grad.7
  144.4 2.2 weight_grad.6
  149.7 6.9 %weight_grad.4 = bf16[4,320,1280]{2,1,0:T(8,128)(2,1)S(1)} custom-call(s32[1]{0:T(128)} %bitcast.1.chip, bf16[4,1024,320]{2,1,0:T(8,128)(2,1)S(1)} %bitcast.51, bf16[512,640]{1,0:T(8,128)(2,1)} %get-tuple-element.10.refs_0_, bf16[512,640]{1,0:T(8,128)(2,1)S(1)} %copy-done.7, bf16[512,640]{1,0:T(8,128)(2,1)} %collective-permute-done.18.refs_2_, ...), custom_call_target="tpu_custom_call" | custom-call | flops 3355443200 | bytes 8519680 | tf_op jit(solution)/shard_map/weight_grad/pallas_call | solution.py:278
  158.6 6.4 %weight_grad.5 = bf16[4,320,1280]{2,1,0:T(8,128)(2,1)S(1)} custom-call(s32[1]{0:T(128)} %bitcast.1.chip, bf16[4,1024,320]{2,1,0:T(8,128)(2,1)S(1)} %bitcast.49, bf16[512,640]{1,0:T(8,128)(2,1)} %get-tuple-element.10.refs_0_, bf16[512,640]{1,0:T(8,128)(2,1)S(1)} %copy-done.7, bf16[512,640]{1,0:T(8,128)(2,1)} %collective-permute-done.18.refs_2_, ...), custom_call_target="tpu_custom_call" | custom-call | flops 3355443200 | bytes 8519680 | tf_op jit(solution)/shard_map/weight_grad/pallas_call | solution.py:278
  171.6 5.0 %collective-permute-done.30 = bf16[320,512]{1,0:T(8,128)(2,1)S(1)} collective-permute-done((bf16[320,512]{1,0:T(8,128)(2,1)S(1)}, bf16[320,512]{1,0:T(8,128)(2,1)S(1)}, u32[]{:S(2)}, u32[]{:S(2)}) %collective-permute-start.30) | collective-permute-done | bytes 327712 | tf_op jit(solution)/shard_map/ppermute | solution.py:301
  177.0 15.8 %collective-permute-done.20 = bf16[320,1280]{1,0:T(8,128)(2,1)S(1)} collective-permute-done((bf16[320,1280]{1,0:T(8,128)(2,1)S(1)}, bf16[320,1280]{1,0:T(8,128)(2,1)S(1)}, u32[]{:S(2)}, u32[]{:S(2)}) %collective-permute-start.20) | collective-permute-done | bytes 819232 | tf_op jit(solution)/shard_map/ppermute | solution.py:301
  195.8 16.0 %collective-permute-done.22 = bf16[320,1280]{1,0:T(8,128)(2,1)S(1)} collective-permute-done((bf16[320,1280]{1,0:T(8,128)(2,1)S(1)}, bf16[320,1280]{1,0:T(8,128)(2,1)S(1)}, u32[]{:S(2)}, u32[]{:S(2)}) %collective-permute-start.22) | collective-permute-done | bytes 819232 | tf_op jit(solution)/shard_map/ppermute | solution.py:301
  212.2 15.7 %collective-permute-done.23 = bf16[320,1280]{1,0:T(8,128)(2,1)S(1)} collective-permute-done((bf16[320,1280]{1,0:T(8,128)(2,1)S(1)}, bf16[320,1280]{1,0:T(8,128)(2,1)S(1)}, u32[]{:S(2)}, u32[]{:S(2)}) %collective-permute-start.23) | collective-permute-done | bytes 819232 | tf_op jit(solution)/shard_map/ppermute | solution.py:301
  229.2 15.6 %collective-permute-done.25 = bf16[320,1280]{1,0:T(8,128)(2,1)S(1)} collective-permute-done((bf16[320,1280]{1,0:T(8,128)(2,1)S(1)}, bf16[320,1280]{1,0:T(8,128)(2,1)S(1)}, u32[]{:S(2)}, u32[]{:S(2)}) %collective-permute-start.25) | collective-permute-done | bytes 819232 | tf_op jit(solution)/shard_map/ppermute | solution.py:301
  (128 shorter events, 47.5 us)
Async XLA Ops:
  7.2 125.1 %all-gather.7.cloned.1.call-start = ((), (), s32[]{:S(2)}) async-start(), calls=%async_computation.3 | async-start | bytes 3932160 | tf_op jit(solution)/shard_map/all_gather | solution.py:353
  12.5 130.0 %all-gather.5.cloned.1.call-start = ((), (), s32[]{:S(2)}) async-start(), calls=%async_computation.2 | async-start | bytes 3932160 | tf_op jit(solution)/shard_map/all_gather | solution.py:353
  17.2 20.0 %collective-permute-start.4 = (bf16[512,512]{1,0:T(8,128)(2,1)S(1)}, bf16[512,512]{1,0:T(8,128)(2,1)S(1)}, u32[]{:S(2)}, u32[]{:S(2)}) collective-permute-start(bf16[512,512]{1,0:T(8,128)(2,1)S(1)} %pad_maximum_fusion.2.refs_0_), channel_id=1, source_target_pairs={{0,4},{4,0},{8,12},{12,8},{16,20},{20,16},{24,28},{28,24},{1,5},{5... | collective-permute-start | bytes 1572872 | tf_op jit(solution)/shard_map/ppermute | solution.py:301
  50.1 21.8 %collective-permute-start.13 = (bf16[2048,256]{1,0:T(8,128)(2,1)}, bf16[2048,256]{1,0:T(8,128)(2,1)S(1)}, u32[]{:S(2)}, u32[]{:S(2)}) collective-permute-start(bf16[2048,256]{1,0:T(8,128)(2,1)} %get-tuple-element.15), channel_id=1, source_target_pairs={{0,4},{4,0},{8,12},{12,8},{16,20},{20,16},{24,28},{28,24},{1,5},{5... | collective-permute-start | bytes 3145736 | tf_op jit(solution)/shard_map/ppermute | solution.py:301
  55.8 190.8 %reduce-scatter.2.cloned.1.call-start = ((), (), s32[]{:S(2)}) async-start(), calls=%async_computation.1 | async-start | bytes 6553600 | tf_op jit(solution)/shard_map/reduce_scatter | solution.py:368
  66.3 23.4 %collective-permute-start.9 = (bf16[2048,256]{1,0:T(8,128)(2,1)}, bf16[2048,256]{1,0:T(8,128)(2,1)S(1)}, u32[]{:S(2)}, u32[]{:S(2)}) collective-permute-start(bf16[2048,256]{1,0:T(8,128)(2,1)} %get-tuple-element.13), channel_id=1, source_target_pairs={{0,4},{4,0},{8,12},{12,8},{16,20},{20,16},{24,28},{28,24},{1,5},{5... | collective-permute-start | bytes 3145736 | tf_op jit(solution)/shard_map/ppermute | solution.py:301
  72.2 23.1 %collective-permute-start.14 = (bf16[512,256]{1,0:T(8,128)(2,1)S(1)}, bf16[512,256]{1,0:T(8,128)(2,1)S(1)}, u32[]{:S(2)}, u32[]{:S(2)}) collective-permute-start(bf16[512,256]{1,0:T(8,128)(2,1)S(1)} %get-tuple-element.32), channel_id=1, source_target_pairs={{0,8},{4,12},{8,0},{12,4},{16,24},{20,28},{24,16},{28,20},{1,9},{5... | collective-permute-start | bytes 786440 | tf_op jit(solution)/shard_map/ppermute | solution.py:301
  88.1 15.8 %collective-permute-start.15 = (bf16[512,256]{1,0:T(8,128)(2,1)S(1)}, bf16[512,256]{1,0:T(8,128)(2,1)S(1)}, u32[]{:S(2)}, u32[]{:S(2)}) collective-permute-start(bf16[512,256]{1,0:T(8,128)(2,1)S(1)} %get-tuple-element.34), channel_id=1, source_target_pairs={{0,16},{4,20},{8,24},{12,28},{16,0},{20,4},{24,8},{28,12},{1,17},{... | collective-permute-start | bytes 786440 | tf_op jit(solution)/shard_map/ppermute | solution.py:301
  88.2 15.8 %collective-permute-start.16 = (bf16[512,256]{1,0:T(8,128)(2,1)S(1)}, bf16[512,256]{1,0:T(8,128)(2,1)S(1)}, u32[]{:S(2)}, u32[]{:S(2)}) collective-permute-start(bf16[512,256]{1,0:T(8,128)(2,1)S(1)} %get-tuple-element.33), channel_id=1, source_target_pairs={{0,24},{4,28},{8,16},{12,20},{16,8},{20,12},{24,0},{28,4},{1,25},{... | collective-permute-start | bytes 786440 | tf_op jit(solution)/shard_map/ppermute | solution.py:301
  90.1 16.5 %collective-permute-start.10 = (bf16[512,256]{1,0:T(8,128)(2,1)S(1)}, bf16[512,256]{1,0:T(8,128)(2,1)S(1)}, u32[]{:S(2)}, u32[]{:S(2)}) collective-permute-start(bf16[512,256]{1,0:T(8,128)(2,1)S(1)} %get-tuple-element.35), channel_id=1, source_target_pairs={{0,8},{4,12},{8,0},{12,4},{16,24},{20,28},{24,16},{28,20},{1,9},{5... | collective-permute-start | bytes 786440 | tf_op jit(solution)/shard_map/ppermute | solution.py:301
  92.1 20.9 %collective-permute-start.11 = (bf16[512,256]{1,0:T(8,128)(2,1)S(1)}, bf16[512,256]{1,0:T(8,128)(2,1)S(1)}, u32[]{:S(2)}, u32[]{:S(2)}) collective-permute-start(bf16[512,256]{1,0:T(8,128)(2,1)S(1)} %get-tuple-element.37), channel_id=1, source_target_pairs={{0,16},{4,20},{8,24},{12,28},{16,0},{20,4},{24,8},{28,12},{1,17},{... | collective-permute-start | bytes 786440 | tf_op jit(solution)/shard_map/ppermute | solution.py:301
  95.3 17.7 %collective-permute-start.12 = (bf16[512,256]{1,0:T(8,128)(2,1)S(1)}, bf16[512,256]{1,0:T(8,128)(2,1)S(1)}, u32[]{:S(2)}, u32[]{:S(2)}) collective-permute-start(bf16[512,256]{1,0:T(8,128)(2,1)S(1)} %get-tuple-element.36), channel_id=1, source_target_pairs={{0,24},{4,28},{8,16},{12,20},{16,8},{20,12},{24,0},{28,4},{1,25},{... | collective-permute-start | bytes 786440 | tf_op jit(solution)/shard_map/ppermute | solution.py:301
  131.0 17.3 %collective-permute-start.18 = (bf16[512,640]{1,0:T(8,128)(2,1)}, bf16[512,640]{1,0:T(8,128)(2,1)}, u32[]{:S(2)}, u32[]{:S(2)}) collective-permute-start(bf16[512,640]{1,0:T(8,128)(2,1)} %get-tuple-element.10.refs_0_), channel_id=1, source_target_pairs={{0,4},{4,0},{8,12},{12,8},{16,20},{20,16},{24,28},{28,24},{1,5},{5... | collective-permute-start | bytes 1966088 | tf_op jit(solution)/shard_map/ppermute | solution.py:301
  137.4 27.6 %collective-permute-start.31 = (bf16[320,512]{1,0:T(8,128)(2,1)}, bf16[320,512]{1,0:T(8,128)(2,1)S(1)}, u32[]{:S(2)}, u32[]{:S(2)}) collective-permute-start(bf16[320,512]{1,0:T(8,128)(2,1)} %get-tuple-element.22), channel_id=1, source_target_pairs={{0,8},{4,12},{8,0},{12,4},{16,24},{20,28},{24,16},{28,20},{1,9},{5... | collective-permute-start | bytes 983048 | tf_op jit(solution)/shard_map/ppermute | solution.py:301
  137.7 27.3 %collective-permute-start.32 = (bf16[320,512]{1,0:T(8,128)(2,1)}, bf16[320,512]{1,0:T(8,128)(2,1)}, u32[]{:S(2)}, u32[]{:S(2)}) collective-permute-start(bf16[320,512]{1,0:T(8,128)(2,1)} %get-tuple-element.24), channel_id=1, source_target_pairs={{0,16},{4,20},{8,24},{12,28},{16,0},{20,4},{24,8},{28,12},{1,17},{... | collective-permute-start | bytes 983048 | tf_op jit(solution)/shard_map/ppermute | solution.py:301
  139.1 27.6 %collective-permute-start.33 = (bf16[320,512]{1,0:T(8,128)(2,1)}, bf16[320,512]{1,0:T(8,128)(2,1)}, u32[]{:S(2)}, u32[]{:S(2)}) collective-permute-start(bf16[320,512]{1,0:T(8,128)(2,1)} %get-tuple-element.23), channel_id=1, source_target_pairs={{0,24},{4,28},{8,16},{12,20},{16,8},{20,12},{24,0},{28,4},{1,25},{... | collective-permute-start | bytes 983048 | tf_op jit(solution)/shard_map/ppermute | solution.py:301
  146.7 22.1 %collective-permute-start.28 = (bf16[320,512]{1,0:T(8,128)(2,1)S(1)}, bf16[320,512]{1,0:T(8,128)(2,1)S(1)}, u32[]{:S(2)}, u32[]{:S(2)}) collective-permute-start(bf16[320,512]{1,0:T(8,128)(2,1)S(1)} %get-tuple-element.25), channel_id=1, source_target_pairs={{0,8},{4,12},{8,0},{12,4},{16,24},{20,28},{24,16},{28,20},{1,9},{5... | collective-permute-start | bytes 983048 | tf_op jit(solution)/shard_map/ppermute | solution.py:301
  148.2 21.9 %collective-permute-start.29 = (bf16[320,512]{1,0:T(8,128)(2,1)S(1)}, bf16[320,512]{1,0:T(8,128)(2,1)S(1)}, u32[]{:S(2)}, u32[]{:S(2)}) collective-permute-start(bf16[320,512]{1,0:T(8,128)(2,1)S(1)} %get-tuple-element.27), channel_id=1, source_target_pairs={{0,16},{4,20},{8,24},{12,28},{16,0},{20,4},{24,8},{28,12},{1,17},{... | collective-permute-start | bytes 983048 | tf_op jit(solution)/shard_map/ppermute | solution.py:301
  165.1 27.7 %collective-permute-start.20 = (bf16[320,1280]{1,0:T(8,128)(2,1)S(1)}, bf16[320,1280]{1,0:T(8,128)(2,1)S(1)}, u32[]{:S(2)}, u32[]{:S(2)}) collective-permute-start(bf16[320,1280]{1,0:T(8,128)(2,1)S(1)} %get-tuple-element.16), channel_id=1, source_target_pairs={{0,8},{4,12},{8,0},{12,4},{16,24},{20,28},{24,16},{28,20},{1,9},{5... | collective-permute-start | bytes 2457608 | tf_op jit(solution)/shard_map/ppermute | solution.py:301
  166.8 29.1 %collective-permute-start.21 = (bf16[320,1280]{1,0:T(8,128)(2,1)S(1)}, bf16[320,1280]{1,0:T(8,128)(2,1)S(1)}, u32[]{:S(2)}, u32[]{:S(2)}) collective-permute-start(bf16[320,1280]{1,0:T(8,128)(2,1)S(1)} %get-tuple-element.18), channel_id=1, source_target_pairs={{0,16},{4,20},{8,24},{12,28},{16,0},{20,4},{24,8},{28,12},{1,17},{... | collective-permute-start | bytes 2457608 | tf_op jit(solution)/shard_map/ppermute | solution.py:301
  168.8 43.0 %collective-permute-start.22 = (bf16[320,1280]{1,0:T(8,128)(2,1)S(1)}, bf16[320,1280]{1,0:T(8,128)(2,1)S(1)}, u32[]{:S(2)}, u32[]{:S(2)}) collective-permute-start(bf16[320,1280]{1,0:T(8,128)(2,1)S(1)} %get-tuple-element.17), channel_id=1, source_target_pairs={{0,24},{4,28},{8,16},{12,20},{16,8},{20,12},{24,0},{28,4},{1,25},{... | collective-permute-start | bytes 2457608 | tf_op jit(solution)/shard_map/ppermute | solution.py:301
  170.1 57.9 %collective-permute-start.23 = (bf16[320,1280]{1,0:T(8,128)(2,1)S(1)}, bf16[320,1280]{1,0:T(8,128)(2,1)S(1)}, u32[]{:S(2)}, u32[]{:S(2)}) collective-permute-start(bf16[320,1280]{1,0:T(8,128)(2,1)S(1)} %get-tuple-element.19), channel_id=1, source_target_pairs={{0,8},{4,12},{8,0},{12,4},{16,24},{20,28},{24,16},{28,20},{1,9},{5... | collective-permute-start | bytes 2457608 | tf_op jit(solution)/shard_map/ppermute | solution.py:301
  176.6 52.5 %collective-permute-start.24 = (bf16[320,1280]{1,0:T(8,128)(2,1)S(1)}, bf16[320,1280]{1,0:T(8,128)(2,1)S(1)}, u32[]{:S(2)}, u32[]{:S(2)}) collective-permute-start(bf16[320,1280]{1,0:T(8,128)(2,1)S(1)} %get-tuple-element.21), channel_id=1, source_target_pairs={{0,16},{4,20},{8,24},{12,28},{16,0},{20,4},{24,8},{28,12},{1,17},{... | collective-permute-start | bytes 2457608 | tf_op jit(solution)/shard_map/ppermute | solution.py:301
  192.8 52.0 %collective-permute-start.25 = (bf16[320,1280]{1,0:T(8,128)(2,1)S(1)}, bf16[320,1280]{1,0:T(8,128)(2,1)S(1)}, u32[]{:S(2)}, u32[]{:S(2)}) collective-permute-start(bf16[320,1280]{1,0:T(8,128)(2,1)S(1)} %get-tuple-element.20), channel_id=1, source_target_pairs={{0,24},{4,28},{8,16},{12,20},{16,8},{20,12},{24,0},{28,4},{1,25},{... | collective-permute-start | bytes 2457608 | tf_op jit(solution)/shard_map/ppermute | solution.py:301
  (35 other events, 271.6 us)
Sparse Core Ops, SparseCore 0:
  12.6 66.1 all-gather.6
  80.3 62.1 all-gather.4
  145.4 92.3 reduce-scatter.1

commit v2 on v1

v2 whole, which is shorter than its diff:
```python
import functools
import math

import jax
import jax.numpy as jnp
from jax import lax
from jax.experimental import pallas as pl
from jax.experimental.pallas import tpu as pltpu
from jax.sharding import PartitionSpec as P

H = 40
KVH = 8
HD = 128
BLK = 128
NGLOB = 2
GROUPS = H // KVH
ROWS = GROUPS * BLK
TURN = 8
SPAN = TURN * BLK
SCALE = 1.0 / math.sqrt(HD)
EXP_SCALE = SCALE * math.log2(math.e)
MASKED = -1e30
BF16 = jnp.bfloat16
F32 = jnp.float32
MIB = 1024 * 1024


def fold_rows(x):
    return x.reshape(x.shape[0] // 8, 8, x.shape[1])


def attn_kernel(places, tok_rows, lists, globs, here, q_ref, do_ref, *refs):
    pieces, refs = refs[: len(places)], refs[len(places) :]
    dq_ref, same_ref, other_ref, kv_ref, s_ref, dp_ref, dqt_ref, dk_acc, dv_acc, ids = refs
    step = pl.program_id(0)
    me = here[0]
    ctx_size = kv_ref.shape[0] // tok_rows

    @pl.when(step == 0)
    def _():
        dk_acc[...] = jnp.zeros_like(dk_acc)
        dv_acc[...] = jnp.zeros_like(dv_acc)
        for mask, piece in zip(places, pieces):
            start = pl.multiple_of((me ^ mask) * tok_rows, BLK)
            kv_ref[pl.ds(start, piece.shape[0]), :] = piece[...]

    blk = me * (tok_rows // BLK) + step
    is_global = globs[0] == blk
    for g in range(1, NGLOB):
        is_global = is_global | (globs[g] == blk)

    def all_before():
        def put(i, carry):
            ids[TURN + i] = i
            return carry

        lax.fori_loop(0, blk, put, 0)
        return blk

    def listed():
        count = jnp.int32(0)
        for slot in range(lists.shape[1]):
            other = lists[step, slot]
            ids[TURN + count] = jnp.maximum(other, 0)
            count = count + jnp.where((other >= 0) & (other != blk), 1, 0)
        for g in range(NGLOB):
            other = globs[g]
            ids[TURN + count] = other
            count = count + jnp.where(other <= blk, 1, 0)
        return count

    count = lax.cond(is_global, all_before, listed)
    extra = lax.rem(count, TURN)
    ids[0] = blk
    for i in range(1, TURN):
        ids[i] = jnp.where(i <= extra, ids[jnp.maximum(TURN + count - i, 0)], blk)
    turns = 1 + lax.div(count, TURN)

    def stacked(ref):
        return jnp.concatenate([ref[:, g * HD : (g + 1) * HD] for g in range(GROUPS)], axis=0)

    q_rows = stacked(q_ref)
    do_rows = stacked(do_ref)
    q_cols = q_rows.T
    do_cols = do_rows.T

    def start_of(i):
        return pl.multiple_of(ids[i] * BLK, BLK)

    def keys_of(p, half):
        cols = slice(half * HD, (half + 1) * HD)
        return jnp.concatenate(
            [kv_ref[pl.ds(start_of(TURN * p + i), BLK), cols] for i in range(TURN)], axis=0
        )

    def at(p):
        return pl.ds(pl.multiple_of(p * SPAN, SPAN), SPAN)

    def scores_of(p):
        return jnp.dot(keys_of(p, 0), q_cols, preferred_element_type=F32)

    key_pos = lax.broadcasted_iota(jnp.int32, (BLK, ROWS), 0)
    query_pos = lax.broadcasted_iota(jnp.int32, (BLK, ROWS), 1) & (BLK - 1)
    scores = scores_of(0)
    parts = [jnp.where(key_pos <= query_pos, scores[:BLK], MASKED)]
    for i in range(1, TURN):
        bias = jnp.where(i <= extra, 0.0, MASKED).astype(F32)
        parts.append(scores[i * BLK : (i + 1) * BLK] + bias)
    scores = jnp.concatenate(parts, axis=0)
    s_ref[at(0), :] = scores
    top8 = jnp.max(fold_rows(scores), axis=0)

    def score_pass(p, top8):
        scores = scores_of(p)
        s_ref[at(p), :] = scores
        return jnp.maximum(top8, jnp.max(fold_rows(scores), axis=0))

    top8 = lax.fori_loop(1, turns, score_pass, top8)
    top = jnp.max(top8, axis=0, keepdims=True)

    def sum_pass(p, carry):
        total8, dot8 = carry
        e = jnp.exp2((s_ref[at(p), :] - top) * EXP_SCALE)
        dp = jnp.dot(keys_of(p, 1), do_cols, preferred_element_type=F32)
        s_ref[at(p), :] = e
        dp_ref[at(p), :] = dp
        return (
            total8 + jnp.sum(fold_rows(e), axis=0),
            dot8 + jnp.sum(fold_rows(e * dp), axis=0),
        )

    zero8 = jnp.zeros((8, ROWS), F32)
    total8, dot8 = lax.fori_loop(0, turns, sum_pass, (zero8, zero8))
    inverse = 1.0 / jnp.sum(total8, axis=0, keepdims=True)
    delta = jnp.sum(dot8, axis=0, keepdims=True) * inverse
    dqt_ref[...] = jnp.zeros_like(dqt_ref)

    def grad_pass(p, carry):
        prob = s_ref[at(p), :] * inverse
        ds = (prob * (dp_ref[at(p), :] - delta)).astype(BF16)
        dv = jnp.dot(prob.astype(BF16), do_rows, preferred_element_type=F32)
        dk = jnp.dot(ds, q_rows, preferred_element_type=F32)
        dqt_ref[...] += jnp.dot(keys_of(p, 0).T, ds, preferred_element_type=F32)
        for i in range(TURN):
            rows = pl.ds(start_of(TURN * p + i), BLK)
            part = slice(i * BLK, (i + 1) * BLK)
            dk_acc[rows, :] += dk[part]
            dv_acc[rows, :] += dv[part]
        return carry

    lax.fori_loop(0, turns, grad_pass, 0)
    dq = (dqt_ref[...] * SCALE).T.astype(BF16)
    for g in range(GROUPS):
        dq_ref[:, g * HD : (g + 1) * HD] = dq[g * BLK : (g + 1) * BLK]

    @pl.when(step == pl.num_programs(0) - 1)
    def _():
        for chip in range(ctx_size // 2):
            out = slice(chip * tok_rows, (chip + 1) * tok_rows)
            for ref, core in ((same_ref, 0), (other_ref, 1)):
                start = pl.multiple_of((me ^ (2 * chip + core)) * tok_rows, BLK)
                rows = pl.ds(start, tok_rows)
                ref[out, :HD] = (dk_acc[rows, :] * SCALE).astype(BF16)
                ref[out, HD:] = dv_acc[rows, :].astype(BF16)


def attention_grads(head, block_lists, global_ids, here, queries, grad_out, places, pieces):
    tok_rows = queries.shape[0]
    blk_count = tok_rows // BLK
    total_rows = sum(piece.shape[0] for piece in pieces)
    slots = max(block_lists.shape[1] + NGLOB + 1, total_rows // BLK // 2)
    slots = -(-slots // TURN) * TURN
    smem = pl.BlockSpec(memory_space=pltpu.SMEM)
    pair_cols = 2 * HD
    work = blk_count * 9 * BLK * ROWS
    half = pl.BlockSpec((total_rows // 2, pair_cols), lambda a: (0, 0))
    half_shape = jax.ShapeDtypeStruct((total_rows // 2, pair_cols), BF16)
    return pl.pallas_call(
        functools.partial(attn_kernel, places, tok_rows),
        grid=(blk_count,),
        in_specs=[
            smem,
            smem,
            smem,
            pl.BlockSpec((BLK, ROWS), lambda a: (a, head)),
            pl.BlockSpec((BLK, ROWS), lambda a: (a, head)),
        ]
        + [
            pl.BlockSpec(piece.shape, lambda a: (0, 0), pipeline_mode=pl.Buffered(1))
            for piece in pieces
        ],
        out_specs=[pl.BlockSpec((BLK, ROWS), lambda a: (a, 0)), half, half],
        out_shape=[jax.ShapeDtypeStruct((tok_rows, ROWS), BF16), half_shape, half_shape],
        scratch_shapes=[
            pltpu.VMEM((total_rows, pair_cols), BF16),
            pltpu.VMEM((slots * BLK, ROWS), F32),
            pltpu.VMEM((slots * BLK, ROWS), F32),
            pltpu.VMEM((HD, ROWS), F32),
            pltpu.VMEM((total_rows, HD), F32),
            pltpu.VMEM((total_rows, HD), F32),
            pltpu.SMEM((slots + TURN + 1,), jnp.int32),
        ],
        compiler_params=pltpu.CompilerParams(
            dimension_semantics=("arbitrary",), vmem_limit_bytes=58 * MIB
        ),
        cost_estimate=pl.CostEstimate(flops=1000, transcendentals=0, bytes_accessed=1000),
        name="attn_grads",
    )(block_lists, global_ids, here, queries, grad_out, *pieces)


def dot_t(rows, weight):
    return lax.dot_general(rows, weight, (((1,), (1,)), ((), ())), preferred_element_type=F32)


def query_term_kernel(heads, *refs):
    dq, (wq_ref, out_ref) = refs[:heads], refs[heads:]
    total = dot_t(dq[0][...], wq_ref[:, :ROWS])
    for j in range(1, heads):
        total += dot_t(dq[j][...], wq_ref[:, j * ROWS : (j + 1) * ROWS])
    out_ref[...] = total.astype(BF16)


def query_term(dq, w_query):
    rows, (width, cols) = dq[0].shape[0], w_query.shape
    tile = width // 4
    return pl.pallas_call(
        functools.partial(query_term_kernel, len(dq)),
        grid=(width // tile,),
        in_specs=[pl.BlockSpec(x.shape, lambda i: (0, 0)) for x in dq]
        + [pl.BlockSpec((tile, cols), lambda i: (i, 0))],
        out_specs=pl.BlockSpec((rows, tile), lambda i: (0, i)),
        out_shape=jax.ShapeDtypeStruct((rows, width), BF16),
        compiler_params=pltpu.CompilerParams(
            dimension_semantics=("arbitrary",), vmem_limit_bytes=58 * MIB
        ),
        cost_estimate=pl.CostEstimate(flops=1000, transcendentals=0, bytes_accessed=1000),
        name="query_term",
    )(*dq, w_query)


def kv_term_kernel(heads, *refs):
    grads, (base_ref, wk_ref, wv_ref, out_ref, dk_ref, dv_ref) = refs[:heads], refs[heads:]

    @pl.when(pl.program_id(0) == 0)
    def _():
        for j in range(heads):
            cols = slice(j * HD, (j + 1) * HD)
            dk_ref[:, cols] = grads[j][:, :HD]
            dv_ref[:, cols] = grads[j][:, HD:]

    total = base_ref[...].astype(F32) + dot_t(dk_ref[...], wk_ref[...]) + dot_t(dv_ref[...], wv_ref[...])
    out_ref[...] = total.astype(BF16)


def with_kv_term(base, dkv, w_key, w_value):
    rows, width = base.shape
    cols = w_key.shape[1]
    tile = width // 4
    weight = pl.BlockSpec((tile, cols), lambda i: (i, 0))
    return pl.pallas_call(
        functools.partial(kv_term_kernel, len(dkv)),
        grid=(width // tile,),
        in_specs=[pl.BlockSpec(x.shape, lambda i: (0, 0)) for x in dkv]
        + [pl.BlockSpec((rows, tile), lambda i: (0, i)), weight, weight],
        out_specs=pl.BlockSpec((rows, tile), lambda i: (0, i)),
        out_shape=jax.ShapeDtypeStruct((rows, width), BF16),
        scratch_shapes=[pltpu.VMEM((rows, cols), BF16)] * 2,
        compiler_params=pltpu.CompilerParams(
            dimension_semantics=("arbitrary",), vmem_limit_bytes=58 * MIB
        ),
        cost_estimate=pl.CostEstimate(flops=1000, transcendentals=0, bytes_accessed=1000),
        name="kv_term",
    )(*dkv, base, w_key, w_value)


def weight_grad_kernel(count, chip, x_ref, *refs):
    out_ref = refs[-1]
    own, partner = refs[:count], refs[count : 2 * count]
    inputs = x_ref[0].T
    rows = own[0].shape[0]
    start = 0
    for mine, theirs in zip(own, partner):
        total = jnp.dot(inputs[:, :rows], mine[...], preferred_element_type=F32)
        total += jnp.dot(inputs[:, rows:], theirs[...], preferred_element_type=F32)
        cols = mine.shape[1]
        out_ref[0, :, start : start + cols] = total.astype(BF16)
        start += cols


def weight_grad(chip, inputs, own, partner):
    chips, rows, width = inputs.shape
    cols = sum(x.shape[1] for x in own)
    return pl.pallas_call(
        functools.partial(weight_grad_kernel, len(own)),
        grid_spec=pltpu.PrefetchScalarGridSpec(
            num_scalar_prefetch=1,
            grid=(chips,),
            in_specs=[pl.BlockSpec((1, rows, width), lambda i, chip: (chip[0] ^ i, 0, 0))]
            + [pl.BlockSpec(x.shape, lambda i, chip: (0, 0)) for x in own + partner],
            out_specs=pl.BlockSpec((1, width, cols), lambda i, chip: (i, 0, 0)),
        ),
        out_shape=jax.ShapeDtypeStruct((chips, width, cols), BF16),
        compiler_params=pltpu.CompilerParams(
            dimension_semantics=("arbitrary",), vmem_limit_bytes=58 * MIB
        ),
        cost_estimate=pl.CostEstimate(flops=1000, transcendentals=0, bytes_accessed=1000),
        name="weight_grad",
    )(chip, inputs, *own, *partner)


def swap(x, mask):
    return lax.ppermute(x, "ctx", [(i, i ^ mask) for i in range(lax.axis_size("ctx"))])


def gather_pieces(x):
    size = lax.axis_size("ctx")
    found = [(0, x)] + [(mask, swap(x, mask)) for mask in range(2, size, 2)]
    return found + [(mask ^ 1, swap(piece, 1)) for mask, piece in found]


def after(x, *others):
    return lax.optimization_barrier((x, others))[0]


def total_of(parts):
    total = parts[0].astype(F32)
    for part in parts[1:]:
        total = total + part.astype(F32)
    return total.astype(BF16)


def scattered(partial):
    chips, rows, _ = partial.shape
    if chips != 4:
        top = total_of([partial[0]] + [swap(partial[i], 2 * i) for i in range(1, chips)])
        return [top]
    half = rows // 2
    by_side, by_front = swap(partial[3, :half], 2), swap(partial[3, half:], 4)
    side_top, front_low = swap(partial[1, :half], 2), swap(partial[2, half:], 4)
    front_top = swap(total_of([partial[2, :half], by_side]), 4)
    side_low = swap(total_of([partial[1, half:], by_front]), 2)
    return [
        total_of([partial[0, :half], side_top, front_top]),
        total_of([partial[0, half:], side_low, front_low]),
    ]


def shards(
    layer_input, w_query, w_key, w_value, queries, keys, values, grad_out, block_lists, global_ids
):
    tok_rows, width = layer_input.shape
    kv_heads = keys.shape[1] // HD
    chips = lax.axis_size("ctx") // 2
    here = lax.axis_index("ctx").astype(jnp.int32)
    core = here % 2
    chip = (here // 2).reshape(1)

    def own_kv(j):
        cols = slice(j * HD, (j + 1) * HD)
        return jnp.concatenate([keys[:, cols], values[:, cols]], axis=1)

    size = lax.axis_size("ctx")
    gathered = [gather_pieces(own_kv(0))]
    arrived = [piece for _, piece in gathered[0]]
    for j in range(1, kv_heads):
        own = after(own_kv(j), *arrived)
        gathered.append([(0, own)] + [(mask, swap(own, mask)) for mask in range(2, size, 2)])

    half = width // 2
    kept = lax.dynamic_slice_in_dim(layer_input, core * half, half, 1)
    given = lax.dynamic_slice_in_dim(layer_input, (1 - core) * half, half, 1)
    input_pair = jnp.concatenate([kept, swap(given, 1)], axis=0)
    inputs = lax.all_gather(input_pair, "tp", axis=0, tiled=False)

    dq, dkv = [], []
    ready = ()
    for j in range(kv_heads):
        dq_j, same, other = attention_grads(
            j,
            block_lists,
            global_ids,
            after(here.reshape(1), *ready),
            queries,
            grad_out,
            [mask for mask, _ in gathered[j]],
            [piece for _, piece in gathered[j]],
        )
        dq.append(dq_j)
        if j + 1 < kv_heads:
            early = [(mask, after(piece, dq_j)) for mask, piece in gathered[j + 1]]
            other = after(other, *[piece for _, piece in early])
            gathered[j + 1] = early + [(mask ^ 1, swap(piece, 1)) for mask, piece in early]
        other = after(other, *dkv)
        chip_sum = total_of([same, swap(other, 1)]).reshape(chips, tok_rows, 2 * HD)
        ready = (chip_sum,)
        if j == kv_heads - 1:
            dq_partner = [swap(x, 1) for x in dq]
            base = query_term(
                [after(dq[0], chip_sum, *dq_partner)] + dq[1:], w_query
            )
            chip_sum_last = after(chip_sum[0], base)
        else:
            chip_sum_last = after(chip_sum[0], *dq)
        dkv.append(
            total_of([chip_sum_last] + [swap(chip_sum[i], 2 * i) for i in range(1, chips)])
        )
    input_term = with_kv_term(base, dkv, w_key, w_value)
    grad_x = lax.psum_scatter(input_term, "tp", scatter_dimension=1, tiled=True)
    dkv_partner = [swap(x, 1) for x in dkv]

    part_query = weight_grad(
        chip, after(inputs, input_term), dq, dq_partner
    )
    part_kv = weight_grad(chip, inputs, [after(dkv[0], part_query)] + dkv[1:], dkv_partner)
    grad_w_query = jnp.concatenate(scattered(part_query), axis=0)
    grad_w_kv = jnp.concatenate(scattered(part_kv), axis=0)

    def columns(first):
        return jnp.concatenate(
            [grad_w_kv[:, c : c + HD] for c in range(first, 2 * HD * kv_heads, 2 * HD)], axis=1
        )

    return (grad_x, grad_w_query, columns(0), columns(HD))


def solution(mesh):
    return jax.shard_map(
        shards,
        mesh=mesh,
        in_specs=(
            P("ctx", "tp"),
            P(None, "tp"),
            P(None, "tp"),
            P(None, "tp"),
            P("ctx", "tp"),
            P("ctx", "tp"),
            P("ctx", "tp"),
            P("ctx", "tp"),
            P("ctx", None),
            P(),
        ),
        out_specs=(P("ctx", "tp"), P("ctx", "tp"), P("ctx", "tp"), P("ctx", "tp")),
        check_vma=False,
    )
```

time: 254 us -> 220 us (0.87)
  waiting for transfers between devices: 112 us -> 77.5 us
  starting transfers between devices: 54.2 us -> 37.7 us
  Pallas kernels: 53.2 us -> 68 us
  other arithmetic: 7.63 us -> 13 us
  local copies, waits for them, and re-layouts: 11.9 us -> 8.25 us
    ppermute x34 -> x39, waiting for transfers between devices: 110 us -> 71.1 us  [swap(): lax.ppermute(x, 'ctx', [(i, i ^ mask) for i in range(lax.axis_size('ctx'))])]
    ppermute x34 -> x39, starting transfers between devices: 53.9 us -> 37.6 us  [swap(): lax.ppermute(x, 'ctx', [(i, i ^ mask) for i in range(lax.axis_size('ctx'))])]
    pallas_call x2, Pallas kernels: 20.7 us -> 27.5 us  [attention_grads(): pl.pallas_call(functools.partial(attn_kernel, places, tok_rows), grid=(bl...]
    pallas_call x1 -> x2, Pallas kernels: 14.8 us -> 21.5 us  [the longest x1 13 us: query_term(): pl.pallas_call(functools.partial(query_term_kernel, len(dq)), grid=(width...]
    unnamed x44 -> x54, local copies, waits for them, and re-layouts: 8.87 us -> 2.96 us
    convert_element_type x8 -> x10, other arithmetic: 3.14 us -> 8.89 us  [total_of(): return total.astype(BF16)]
    all_gather x2 -> x1, waiting for transfers between devices: 1.63 us -> 6.41 us  [shards(): inputs = lax.all_gather(input_pair, 'tp', axis=0, tiled=False)]
    pallas_call x4 -> x2, Pallas kernels: 17.8 us -> 19 us  [weight_grad(): pl.pallas_call(functools.partial(weight_grad_kernel, len(own)), grid_spec...]
  transfers between devices with their start and end apart: 37 -> 41, of which waited for: 19 -> 15; matrix products, arithmetic and copies ran while one was open for 3% -> 7% of each run, Pallas kernels for 21% -> 31%
where the time goes in v2:
time: 220 us; the launch traced here: 219 us
  waiting for transfers between devices  77.5 us (35%)
  Pallas kernels  68 us (31%)
  starting transfers between devices  37.7 us (17%)
  between operations  14.5 us (7%)
  other arithmetic  13 us (6%)
  local copies, waits for them, and re-layouts  8.25 us (4%)
    ppermute x39, waiting for transfers between devices, swap(): lax.ppermute(x, 'ctx', [(i, i ^ mask) for i in range(lax.axis_size('ctx'))])  71.1 us
    ppermute x39, starting transfers between devices, swap(): lax.ppermute(x, 'ctx', [(i, i ^ mask) for i in range(lax.axis_size('ctx'))])  37.6 us
    pallas_call x2, Pallas kernels, attention_grads(): pl.pallas_call(functools.partial(attn_kernel, places, tok_rows), grid=(bl...  27.5 us
    pallas_call x2, Pallas kernels, weight_grad(): pl.pallas_call(functools.partial(weight_grad_kernel, len(own)), grid_spec...  19 us
    pallas_call x1, Pallas kernels, query_term(): pl.pallas_call(functools.partial(query_term_kernel, len(dq)), grid=(width...  13 us
    convert_element_type x10, other arithmetic, total_of(): return total.astype(BF16)  8.89 us
    pallas_call x1, Pallas kernels, with_kv_term(): pl.pallas_call(functools.partial(kv_term_kernel, len(dkv)), grid=(width /...  8.51 us
    all_gather x1, waiting for transfers between devices, shards(): inputs = lax.all_gather(input_pair, 'tp', axis=0, tiled=False)  6.41 us
  transfers between devices with their start and end apart: 41, of which 15 were waited for; matrix products, arithmetic and copies ran while one was open for 7% of the time, Pallas kernels for 31%

profile of v2, /device:TPU:0, one launch (start us, length us, event | category | flops | bytes accessed | tf_op | source)
XLA Modules:
  0.0 219.0 jit_solution(14572260748830676182)
XLA Ops:
  9.2 1.7 collective-permute-done.24
  12.3 2.9 %collective-permute-start = (bf16[512,256]{1,0:T(8,128)(2,1)S(1)}, bf16[512,256]{1,0:T(8,128)(2,1)S(1)}, u32[]{:S(2)}, u32[]{:S(2)}) collective-permute-start(bf16[512,256]{1,0:T(8,128)(2,1)S(1)} %pad_maximum_fusion.3.refs_0_), channel_id=1, source_target_pairs={{0,8},{4,12},{8,0},{12,4},{16,24},{20,28},{24,16},{28,20},{1,9},{5... | collective-permute-start | bytes 786440 | tf_op jit(solution)/shard_map/ppermute | solution.py:312
  16.8 5.5 %collective-permute-done.refs_1_ = bf16[512,256]{1,0:T(8,128)(2,1)S(1)} collective-permute-done((bf16[512,256]{1,0:T(8,128)(2,1)S(1)}, bf16[512,256]{1,0:T(8,128)(2,1)S(1)}, u32[]{:S(2)}, u32[]{:S(2)}) %collective-permute-start) | collective-permute-done | bytes 262176 | tf_op jit(solution)/shard_map/ppermute | solution.py:312
  22.3 6.6 %collective-permute-done.1.refs_2_ = bf16[512,256]{1,0:T(8,128)(2,1)S(1)} collective-permute-done((bf16[512,256]{1,0:T(8,128)(2,1)S(1)}, bf16[512,256]{1,0:T(8,128)(2,1)S(1)}, u32[]{:S(2)}, u32[]{:S(2)}) %collective-permute-start.1) | collective-permute-done | bytes 262176 | tf_op jit(solution)/shard_map/ppermute | solution.py:312
  34.4 13.7 %attn_grads.2 = (bf16[512,640]{1,0:T(8,128)(2,1)}, bf16[2048,256]{1,0:T(8,128)(2,1)}, bf16[2048,256]{1,0:T(8,128)(2,1)}) custom-call(s32[4,6]{1,0:T(4,128)} %lists.3, s32[2]{0:T(128)} %globs.3, s32[1]{0:T(128)} %bitcast.here, bf16[512,1280]{1,0:T(8,128)(2,1)} %q_ref.3, bf16[512,1280]{1,0:T(8,128)(2,1)} %do_ref.3, bf16[512,256]{1,0:T(8,128)(2,1)} %copy-done.6, ...), custom_call_target="tpu_custom_call" | custom-call | flops 1000 | bytes 1000 | tf_op jit(solution)/shard_map/attn_grads/pallas_call | solution.py:178
  49.4 2.4 %collective-permute-done.10 = bf16[2048,256]{1,0:T(8,128)(2,1)S(1)} collective-permute-done((bf16[2048,256]{1,0:T(8,128)(2,1)}, bf16[2048,256]{1,0:T(8,128)(2,1)S(1)}, u32[]{:S(2)}, u32[]{:S(2)}) %collective-permute-start.10) | collective-permute-done | bytes 1048608 | tf_op jit(solution)/shard_map/ppermute | solution.py:312
  53.4 1.6 collective-permute-start.13
  55.0 3.1 %collective-permute-start.12 = (bf16[512,256]{1,0:T(8,128)(2,1)S(1)}, bf16[512,256]{1,0:T(8,128)(2,1)S(1)}, u32[]{:S(2)}, u32[]{:S(2)}) collective-permute-start(bf16[512,256]{1,0:T(8,128)(2,1)S(1)} %get-tuple-element.60), channel_id=1, source_target_pairs={{0,16},{4,20},{8,24},{12,28},{16,0},{20,4},{24,8},{28,12},{1,17},{... | collective-permute-start | bytes 786440 | tf_op jit(solution)/shard_map/ppermute | solution.py:312
  59.6 13.7 %attn_grads.3 = (bf16[512,640]{1,0:T(8,128)(2,1)}, bf16[2048,256]{1,0:T(8,128)(2,1)}, bf16[2048,256]{1,0:T(8,128)(2,1)}) custom-call(s32[4,6]{1,0:T(4,128)} %lists.3, s32[2]{0:T(128)} %globs.3, s32[1]{0:T(128)} %bitcast.here, bf16[512,1280]{1,0:T(8,128)(2,1)} %q_ref.3, bf16[512,1280]{1,0:T(8,128)(2,1)} %do_ref.3, bf16[512,256]{1,0:T(8,128)(2,1)} %copy-done.5, ...), custom_call_target="tpu_custom_call" | custom-call | flops 1000 | bytes 1000 | tf_op jit(solution)/shard_map/attn_grads/pallas_call | solution.py:178
  74.7 3.3 %collective-permute-done.18 = bf16[2048,256]{1,0:T(8,128)(2,1)S(1)} collective-permute-done((bf16[2048,256]{1,0:T(8,128)(2,1)}, bf16[2048,256]{1,0:T(8,128)(2,1)S(1)}, u32[]{:S(2)}, u32[]{:S(2)}) %collective-permute-start.18) | collective-permute-done | bytes 1048608 | tf_op jit(solution)/shard_map/ppermute | solution.py:312
  79.9 4.2 %collective-permute-start.22 = (bf16[512,256]{1,0:T(8,128)(2,1)S(1)}, bf16[512,256]{1,0:T(8,128)(2,1)S(1)}, u32[]{:S(2)}, u32[]{:S(2)}) collective-permute-start(bf16[512,256]{1,0:T(8,128)(2,1)S(1)} %get-tuple-element.56), channel_id=1, source_target_pairs={{0,16},{4,20},{8,24},{12,28},{16,0},{20,4},{24,8},{28,12},{1,17},{... | collective-permute-start | bytes 786440 | tf_op jit(solution)/shard_map/ppermute | solution.py:312
  84.1 13.0 %query_term.1.refs_2_ = bf16[512,5120]{1,0:T(8,128)(2,1)} custom-call(bf16[512,640]{1,0:T(8,128)(2,1)} %get-tuple-element.36.refs_0_, bf16[512,640]{1,0:T(8,128)(2,1)} %get-tuple-element.35.refs_1_, bf16[5120,1280]{1,0:T(8,128)(2,1)} %refs_2_.1), custom_call_target="tpu_custom_call" | custom-call | flops 1000 | bytes 1000 | tf_op jit(solution)/shard_map/query_term/pallas_call | solution.py:226
  98.0 8.5 %kv_term.1 = bf16[512,5120]{1,0:T(8,128)(2,1)} custom-call(bf16[512,256]{1,0:T(8,128)(2,1)} %add_convert_fusion.3.refs_0_, bf16[512,256]{1,0:T(8,128)(2,1)} %add_convert_fusion.2.refs_1_, bf16[512,5120]{1,0:T(8,128)(2,1)} %query_term.1.refs_2_, bf16[5120,256]{1,0:T(8,128)(2,1)} %refs_3_.1, bf16[5120,256]{1,0:T(8,128)(2,1)} %refs_4_.1), custom_call_target="tpu_custom_call" | custom-call | flops 1000 | bytes 1000 | tf_op jit(solution)/shard_map/kv_term/pallas_call | solution.py:260
  106.5 6.4 %all-gather.3.cloned.1.call-done = bf16[4096,640]{1,0:T(8,128)(2,1)} async-done(((bf16[1024,640]{1,0:T(8,128)(2,1)}), bf16[4096,640]{1,0:T(8,128)(2,1)}) %all-gather.3.cloned.1.call-update) | async-done | bytes 5242896 | tf_op jit(solution)/shard_map/all_gather | solution.py:373
  112.9 12.3 %weight_grad.2 = bf16[4,640,1280]{2,1,0:T(8,128)(2,1)} custom-call(s32[1]{0:T(128)} %bitcast.1.chip, bf16[4,1024,640]{2,1,0:T(8,128)(2,1)} %bitcast.59, bf16[512,640]{1,0:T(8,128)(2,1)} %get-tuple-element.36.refs_0_, bf16[512,640]{1,0:T(8,128)(2,1)} %get-tuple-element.35.refs_1_, bf16[512,640]{1,0:T(8,128)(2,1)} %copy-done.7, bf16[512,640]{1,0:T(8,128)(2,1)} %copy-done.8), custom_call_target="tpu_custom_call" | custom-call | flops 1000 | bytes 1000 | tf_op jit(solution)/shard_map/weight_grad/pallas_call | solution.py:293
  125.2 2.2 slice_bitcast_fusion.6
  132.8 6.8 %weight_grad.3 = bf16[4,640,512]{2,1,0:T(8,128)(2,1)} custom-call(s32[1]{0:T(128)} %bitcast.1.chip, bf16[4,1024,640]{2,1,0:T(8,128)(2,1)} %bitcast.60, bf16[512,256]{1,0:T(8,128)(2,1)} %add_convert_fusion.3.refs_0_, bf16[512,256]{1,0:T(8,128)(2,1)} %add_convert_fusion.2.refs_1_, bf16[512,256]{1,0:T(8,128)(2,1)} %copy-done.23, bf16[512,256]{1,0:T(8,128)(2,1)} %copy-done.24), custom_call_target="tpu_custom_call" | custom-call | flops 1000 | bytes 1000 | tf_op jit(solution)/shard_map/weight_grad/pallas_call | solution.py:293
  143.2 5.3 %collective-permute-done.26 = bf16[320,1280]{1,0:T(8,128)(2,1)S(1)} collective-permute-done((bf16[320,1280]{1,0:T(8,128)(2,1)S(1)}, bf16[320,1280]{1,0:T(8,128)(2,1)S(1)}, u32[]{:S(2)}, u32[]{:S(2)}) %collective-permute-start.26) | collective-permute-done | bytes 819232 | tf_op jit(solution)/shard_map/ppermute | solution.py:312
  151.3 12.6 %collective-permute-done.36 = bf16[320,512]{1,0:T(8,128)(2,1)S(1)} collective-permute-done((bf16[320,512]{1,0:T(8,128)(2,1)S(1)}, bf16[320,512]{1,0:T(8,128)(2,1)S(1)}, u32[]{:S(2)}, u32[]{:S(2)}) %collective-permute-start.36) | collective-permute-done | bytes 327712 | tf_op jit(solution)/shard_map/ppermute | solution.py:312
  167.1 6.0 %collective-permute-done.34 = bf16[320,512]{1,0:T(8,128)(2,1)S(1)} collective-permute-done((bf16[320,512]{1,0:T(8,128)(2,1)S(1)}, bf16[320,512]{1,0:T(8,128)(2,1)S(1)}, u32[]{:S(2)}, u32[]{:S(2)}) %collective-permute-start.34) | collective-permute-done | bytes 327712 | tf_op jit(solution)/shard_map/ppermute | solution.py:312
  174.6 4.6 %collective-permute-done.37 = bf16[320,512]{1,0:T(8,128)(2,1)S(1)} collective-permute-done((bf16[320,512]{1,0:T(8,128)(2,1)S(1)}, bf16[320,512]{1,0:T(8,128)(2,1)S(1)}, u32[]{:S(2)}, u32[]{:S(2)}) %collective-permute-start.37) | collective-permute-done | bytes 327712 | tf_op jit(solution)/shard_map/ppermute | solution.py:312
  182.4 2.7 %collective-permute-done.27 = bf16[320,1280]{1,0:T(8,128)(2,1)S(1)} collective-permute-done((bf16[320,1280]{1,0:T(8,128)(2,1)S(1)}, bf16[320,1280]{1,0:T(8,128)(2,1)S(1)}, u32[]{:S(2)}, u32[]{:S(2)}) %collective-permute-start.27) | collective-permute-done | bytes 819232 | tf_op jit(solution)/shard_map/ppermute | solution.py:312
  185.1 2.1 fusion.5
  189.8 17.9 %collective-permute-done.35 = bf16[320,512]{1,0:T(8,128)(2,1)S(1)} collective-permute-done((bf16[320,512]{1,0:T(8,128)(2,1)S(1)}, bf16[320,512]{1,0:T(8,128)(2,1)S(1)}, u32[]{:S(2)}, u32[]{:S(2)}) %collective-permute-start.35) | collective-permute-done | bytes 327712 | tf_op jit(solution)/shard_map/ppermute | solution.py:312
  (143 shorter events, 45.4 us)
Async XLA Ops:
  7.2 105.8 %all-gather.3.cloned.1.call-start = ((), (), s32[]{:S(2)}) async-start(), calls=%async_computation.2 | async-start | bytes 6553600 | tf_op jit(solution)/shard_map/all_gather | solution.py:373
  12.1 200.1 %reduce-scatter.2.cloned.1.call-start = ((), (), s32[]{:S(2)}) async-start(), calls=%async_computation.1 | async-start | bytes 6553600 | tf_op jit(solution)/shard_map/reduce_scatter | solution.py:408
  15.2 13.7 %collective-permute-start.1 = (bf16[512,256]{1,0:T(8,128)(2,1)S(1)}, bf16[512,256]{1,0:T(8,128)(2,1)S(1)}, u32[]{:S(2)}, u32[]{:S(2)}) collective-permute-start(bf16[512,256]{1,0:T(8,128)(2,1)S(1)} %pad_maximum_fusion.3.refs_0_), channel_id=1, source_target_pairs={{0,16},{4,20},{8,24},{12,28},{16,0},{20,4},{24,8},{28,12},{1,17},{... | collective-permute-start | bytes 786440 | tf_op jit(solution)/shard_map/ppermute | solution.py:312
  16.8 12.7 %collective-permute-start.3 = (bf16[512,256]{1,0:T(8,128)(2,1)S(1)}, bf16[512,256]{1,0:T(8,128)(2,1)S(1)}, u32[]{:S(2)}, u32[]{:S(2)}) collective-permute-start(bf16[512,256]{1,0:T(8,128)(2,1)S(1)} %pad_maximum_fusion.3.refs_0_), channel_id=1, source_target_pairs={{0,4},{4,0},{8,12},{12,8},{16,20},{20,16},{24,28},{28,24},{1,5},{5... | collective-permute-start | bytes 786440 | tf_op jit(solution)/shard_map/ppermute | solution.py:312
  30.8 17.3 %collective-permute-start.7 = (bf16[512,256]{1,0:T(8,128)(2,1)S(1)}, bf16[512,256]{1,0:T(8,128)(2,1)S(1)}, u32[]{:S(2)}, u32[]{:S(2)}) collective-permute-start(bf16[512,256]{1,0:T(8,128)(2,1)S(1)} %pad_maximum_fusion.4.refs_0_), channel_id=1, source_target_pairs={{0,8},{4,12},{8,0},{12,4},{16,24},{20,28},{24,16},{28,20},{1,9},{5... | collective-permute-start | bytes 786440 | tf_op jit(solution)/shard_map/ppermute | solution.py:312
  31.7 16.4 %collective-permute-start.8 = (bf16[512,256]{1,0:T(8,128)(2,1)S(1)}, bf16[512,256]{1,0:T(8,128)(2,1)S(1)}, u32[]{:S(2)}, u32[]{:S(2)}) collective-permute-start(bf16[512,256]{1,0:T(8,128)(2,1)S(1)} %pad_maximum_fusion.4.refs_0_), channel_id=1, source_target_pairs={{0,16},{4,20},{8,24},{12,28},{16,0},{20,4},{24,8},{28,12},{1,17},{... | collective-permute-start | bytes 786440 | tf_op jit(solution)/shard_map/ppermute | solution.py:312
  32.9 15.3 %collective-permute-start.9 = (bf16[512,256]{1,0:T(8,128)(2,1)S(1)}, bf16[512,256]{1,0:T(8,128)(2,1)S(1)}, u32[]{:S(2)}, u32[]{:S(2)}) collective-permute-start(bf16[512,256]{1,0:T(8,128)(2,1)S(1)} %pad_maximum_fusion.4.refs_0_), channel_id=1, source_target_pairs={{0,24},{4,28},{8,16},{12,20},{16,8},{20,12},{24,0},{28,4},{1,25},{... | collective-permute-start | bytes 786440 | tf_op jit(solution)/shard_map/ppermute | solution.py:312
  53.4 19.9 %collective-permute-start.13 = (bf16[512,256]{1,0:T(8,128)(2,1)S(1)}, bf16[512,256]{1,0:T(8,128)(2,1)S(1)}, u32[]{:S(2)}, u32[]{:S(2)}) collective-permute-start(bf16[512,256]{1,0:T(8,128)(2,1)S(1)} %get-tuple-element.59), channel_id=1, source_target_pairs={{0,24},{4,28},{8,16},{12,20},{16,8},{20,12},{24,0},{28,4},{1,25},{... | collective-permute-start | bytes 786440 | tf_op jit(solution)/shard_map/ppermute | solution.py:312
  55.0 18.4 %collective-permute-start.12 = (bf16[512,256]{1,0:T(8,128)(2,1)S(1)}, bf16[512,256]{1,0:T(8,128)(2,1)S(1)}, u32[]{:S(2)}, u32[]{:S(2)}) collective-permute-start(bf16[512,256]{1,0:T(8,128)(2,1)S(1)} %get-tuple-element.60), channel_id=1, source_target_pairs={{0,16},{4,20},{8,24},{12,28},{16,0},{20,4},{24,8},{28,12},{1,17},{... | collective-permute-start | bytes 786440 | tf_op jit(solution)/shard_map/ppermute | solution.py:312
  58.0 15.3 %collective-permute-start.11 = (bf16[512,256]{1,0:T(8,128)(2,1)S(1)}, bf16[512,256]{1,0:T(8,128)(2,1)S(1)}, u32[]{:S(2)}, u32[]{:S(2)}) collective-permute-start(bf16[512,256]{1,0:T(8,128)(2,1)S(1)} %get-tuple-element.61), channel_id=1, source_target_pairs={{0,8},{4,12},{8,0},{12,4},{16,24},{20,28},{24,16},{28,20},{1,9},{5... | collective-permute-start | bytes 786440 | tf_op jit(solution)/shard_map/ppermute | solution.py:312
  78.3 18.8 %collective-permute-start.23 = (bf16[512,256]{1,0:T(8,128)(2,1)S(1)}, bf16[512,256]{1,0:T(8,128)(2,1)S(1)}, u32[]{:S(2)}, u32[]{:S(2)}) collective-permute-start(bf16[512,256]{1,0:T(8,128)(2,1)S(1)} %get-tuple-element.55), channel_id=1, source_target_pairs={{0,24},{4,28},{8,16},{12,20},{16,8},{20,12},{24,0},{28,4},{1,25},{... | collective-permute-start | bytes 786440 | tf_op jit(solution)/shard_map/ppermute | solution.py:312
  79.9 17.2 %collective-permute-start.22 = (bf16[512,256]{1,0:T(8,128)(2,1)S(1)}, bf16[512,256]{1,0:T(8,128)(2,1)S(1)}, u32[]{:S(2)}, u32[]{:S(2)}) collective-permute-start(bf16[512,256]{1,0:T(8,128)(2,1)S(1)} %get-tuple-element.56), channel_id=1, source_target_pairs={{0,16},{4,20},{8,24},{12,28},{16,0},{20,4},{24,8},{28,12},{1,17},{... | collective-permute-start | bytes 786440 | tf_op jit(solution)/shard_map/ppermute | solution.py:312
  84.0 13.1 %collective-permute-start.21 = (bf16[512,256]{1,0:T(8,128)(2,1)S(1)}, bf16[512,256]{1,0:T(8,128)(2,1)S(1)}, u32[]{:S(2)}, u32[]{:S(2)}) collective-permute-start(bf16[512,256]{1,0:T(8,128)(2,1)S(1)} %get-tuple-element.57), channel_id=1, source_target_pairs={{0,8},{4,12},{8,0},{12,4},{16,24},{20,28},{24,16},{28,20},{1,9},{5... | collective-permute-start | bytes 786440 | tf_op jit(solution)/shard_map/ppermute | solution.py:312
  127.3 21.2 %collective-permute-start.26 = (bf16[320,1280]{1,0:T(8,128)(2,1)S(1)}, bf16[320,1280]{1,0:T(8,128)(2,1)S(1)}, u32[]{:S(2)}, u32[]{:S(2)}) collective-permute-start(bf16[320,1280]{1,0:T(8,128)(2,1)S(1)} %get-tuple-element.45), channel_id=1, source_target_pairs={{0,8},{4,12},{8,0},{12,4},{16,24},{20,28},{24,16},{28,20},{1,9},{5... | collective-permute-start | bytes 2457608 | tf_op jit(solution)/shard_map/ppermute | solution.py:312
  129.4 51.5 %collective-permute-start.25 = (bf16[320,1280]{1,0:T(8,128)(2,1)S(1)}, bf16[320,1280]{1,0:T(8,128)(2,1)S(1)}, u32[]{:S(2)}, u32[]{:S(2)}) collective-permute-start(bf16[320,1280]{1,0:T(8,128)(2,1)S(1)} %get-tuple-element.42), channel_id=1, source_target_pairs={{0,8},{4,12},{8,0},{12,4},{16,24},{20,28},{24,16},{28,20},{1,9},{5... | collective-permute-start | bytes 2457608 | tf_op jit(solution)/shard_map/ppermute | solution.py:312
  129.9 52.5 %collective-permute-start.28 = (bf16[320,1280]{1,0:T(8,128)(2,1)S(1)}, bf16[320,1280]{1,0:T(8,128)(2,1)}, u32[]{:S(2)}, u32[]{:S(2)}) collective-permute-start(bf16[320,1280]{1,0:T(8,128)(2,1)S(1)} %get-tuple-element.44), channel_id=1, source_target_pairs={{0,16},{4,20},{8,24},{12,28},{16,0},{20,4},{24,8},{28,12},{1,17},{... | collective-permute-start | bytes 2457608 | tf_op jit(solution)/shard_map/ppermute | solution.py:312
  141.1 24.4 %collective-permute-start.38 = (bf16[320,512]{1,0:T(8,128)(2,1)S(1)}, bf16[320,512]{1,0:T(8,128)(2,1)S(1)}, u32[]{:S(2)}, u32[]{:S(2)}) collective-permute-start(bf16[320,512]{1,0:T(8,128)(2,1)S(1)} %get-tuple-element.49), channel_id=1, source_target_pairs={{0,16},{4,20},{8,24},{12,28},{16,0},{20,4},{24,8},{28,12},{1,17},{... | collective-permute-start | bytes 983048 | tf_op jit(solution)/shard_map/ppermute | solution.py:312
  141.7 22.2 %collective-permute-start.36 = (bf16[320,512]{1,0:T(8,128)(2,1)S(1)}, bf16[320,512]{1,0:T(8,128)(2,1)S(1)}, u32[]{:S(2)}, u32[]{:S(2)}) collective-permute-start(bf16[320,512]{1,0:T(8,128)(2,1)S(1)} %get-tuple-element.48), channel_id=1, source_target_pairs={{0,16},{4,20},{8,24},{12,28},{16,0},{20,4},{24,8},{28,12},{1,17},{... | collective-permute-start | bytes 983048 | tf_op jit(solution)/shard_map/ppermute | solution.py:312
  148.5 24.6 %collective-permute-start.34 = (bf16[320,512]{1,0:T(8,128)(2,1)S(1)}, bf16[320,512]{1,0:T(8,128)(2,1)S(1)}, u32[]{:S(2)}, u32[]{:S(2)}) collective-permute-start(bf16[320,512]{1,0:T(8,128)(2,1)S(1)} %get-tuple-element.50), channel_id=1, source_target_pairs={{0,8},{4,12},{8,0},{12,4},{16,24},{20,28},{24,16},{28,20},{1,9},{5... | collective-permute-start | bytes 983048 | tf_op jit(solution)/shard_map/ppermute | solution.py:312
  163.9 21.2 %collective-permute-start.27 = (bf16[320,1280]{1,0:T(8,128)(2,1)S(1)}, bf16[320,1280]{1,0:T(8,128)(2,1)S(1)}, u32[]{:S(2)}, u32[]{:S(2)}) collective-permute-start(bf16[320,1280]{1,0:T(8,128)(2,1)S(1)} %fusion.3), channel_id=1, source_target_pairs={{0,16},{4,20},{8,24},{12,28},{16,0},{20,4},{24,8},{28,12},{1,17},{... | collective-permute-start | bytes 2457608 | tf_op jit(solution)/shard_map/ppermute | solution.py:312
  165.5 13.6 %collective-permute-start.37 = (bf16[320,512]{1,0:T(8,128)(2,1)S(1)}, bf16[320,512]{1,0:T(8,128)(2,1)S(1)}, u32[]{:S(2)}, u32[]{:S(2)}) collective-permute-start(bf16[320,512]{1,0:T(8,128)(2,1)S(1)} %fusion.8), channel_id=1, source_target_pairs={{0,8},{4,12},{8,0},{12,4},{16,24},{20,28},{24,16},{28,20},{1,9},{5... | collective-permute-start | bytes 983048 | tf_op jit(solution)/shard_map/ppermute | solution.py:312
  173.1 36.3 %collective-permute-start.30 = (bf16[320,1280]{1,0:T(8,128)(2,1)S(1)}, bf16[320,1280]{1,0:T(8,128)(2,1)S(1)}, u32[]{:S(2)}, u32[]{:S(2)}) collective-permute-start(bf16[320,1280]{1,0:T(8,128)(2,1)S(1)} %get-tuple-element.43), channel_id=1, source_target_pairs={{0,16},{4,20},{8,24},{12,28},{16,0},{20,4},{24,8},{28,12},{1,17},{... | collective-permute-start | bytes 2457608 | tf_op jit(solution)/shard_map/ppermute | solution.py:312
  180.9 26.8 %collective-permute-start.35 = (bf16[320,512]{1,0:T(8,128)(2,1)S(1)}, bf16[320,512]{1,0:T(8,128)(2,1)S(1)}, u32[]{:S(2)}, u32[]{:S(2)}) collective-permute-start(bf16[320,512]{1,0:T(8,128)(2,1)S(1)} %get-tuple-element.47), channel_id=1, source_target_pairs={{0,16},{4,20},{8,24},{12,28},{16,0},{20,4},{24,8},{28,12},{1,17},{... | collective-permute-start | bytes 983048 | tf_op jit(solution)/shard_map/ppermute | solution.py:312
  187.2 22.2 %collective-permute-start.29 = (bf16[320,1280]{1,0:T(8,128)(2,1)S(1)}, bf16[320,1280]{1,0:T(8,128)(2,1)S(1)}, u32[]{:S(2)}, u32[]{:S(2)}) collective-permute-start(bf16[320,1280]{1,0:T(8,128)(2,1)S(1)} %get-tuple-element.41), channel_id=1, source_target_pairs={{0,8},{4,12},{8,0},{12,4},{16,24},{20,28},{24,16},{28,20},{1,9},{5... | collective-permute-start | bytes 2457608 | tf_op jit(solution)/shard_map/ppermute | solution.py:312
  (44 other events, 297.2 us)
Sparse Core Ops, SparseCore 0:
  12.2 100.6 all-gather.2
  115.8 92.1 reduce-scatter.1

commit v3 on v2

--- a/solution.py
+++ b/solution.py
@@ -352,8 +352,8 @@
     kv_heads = keys.shape[1] // HD
     chips = lax.axis_size("ctx") // 2
     here = lax.axis_index("ctx").astype(jnp.int32)
-    core = here % 2
-    chip = (here // 2).reshape(1)
+    core = here & 1
+    chip = (here >> 1).reshape(1)
 
     def own_kv(j):
         cols = slice(j * HD, (j + 1) * HD)
@@ -367,8 +367,12 @@
         gathered.append([(0, own)] + [(mask, swap(own, mask)) for mask in range(2, size, 2)])
 
     half = width // 2
-    kept = lax.dynamic_slice_in_dim(layer_input, core * half, half, 1)
-    given = lax.dynamic_slice_in_dim(layer_input, (1 - core) * half, half, 1)
+    kept, given = (
+        lax.dynamic_slice(
+            layer_input, (0, start * half), (tok_rows, half), allow_negative_indices=False
+        )
+        for start in (core, 1 - core)
+    )
     input_pair = jnp.concatenate([kept, swap(given, 1)], axis=0)
     inputs = lax.all_gather(input_pair, "tp", axis=0, tiled=False)
 

time: 220 us -> 220 us (level)
  starting transfers between devices: 37.7 us -> 40.6 us
  waiting for transfers between devices: 77.5 us -> 74.7 us
    ppermute x39, starting transfers between devices: 37.6 us -> 40.5 us  [swap(): lax.ppermute(x, 'ctx', [(i, i ^ mask) for i in range(lax.axis_size('ctx'))])]
    all_gather x1, waiting for transfers between devices: 6.41 us -> 3.62 us  [shards(): inputs = lax.all_gather(input_pair, 'tp', axis=0, tiled=False)]
where the time goes in v3:
time: 220 us; the launch traced here: 219 us
  waiting for transfers between devices  74.7 us (34%)
  Pallas kernels  68 us (31%)
  starting transfers between devices  40.6 us (18%)
  between operations  14.5 us (7%)
  other arithmetic  13 us (6%)
  local copies, waits for them, and re-layouts  8.25 us (4%)
    ppermute x39, waiting for transfers between devices, swap(): lax.ppermute(x, 'ctx', [(i, i ^ mask) for i in range(lax.axis_size('ctx'))])  71.1 us
    ppermute x39, starting transfers between devices, swap(): lax.ppermute(x, 'ctx', [(i, i ^ mask) for i in range(lax.axis_size('ctx'))])  40.5 us
    pallas_call x2, Pallas kernels, attention_grads(): pl.pallas_call(functools.partial(attn_kernel, places, tok_rows), grid=(bl...  27.5 us
    pallas_call x2, Pallas kernels, weight_grad(): pl.pallas_call(functools.partial(weight_grad_kernel, len(own)), grid_spec...  19 us
    pallas_call x1, Pallas kernels, query_term(): pl.pallas_call(functools.partial(query_term_kernel, len(dq)), grid=(width...  13 us
    convert_element_type x10, other arithmetic, total_of(): return total.astype(BF16)  8.89 us
    pallas_call x1, Pallas kernels, with_kv_term(): pl.pallas_call(functools.partial(kv_term_kernel, len(dkv)), grid=(width /...  8.51 us
  transfers between devices with their start and end apart: 41, of which 15 were waited for; matrix products, arithmetic and copies ran while one was open for 7% of the time, Pallas kernels for 31%

profile of v3, /device:TPU:0, one launch (start us, length us, event | category | flops | bytes accessed | tf_op | source)
XLA Modules:
  0.0 219.0 jit_solution(12244857420323761929)
XLA Ops:
  9.1 1.7 collective-permute-done.24
  12.3 2.9 %collective-permute-start = (bf16[512,256]{1,0:T(8,128)(2,1)S(1)}, bf16[512,256]{1,0:T(8,128)(2,1)S(1)}, u32[]{:S(2)}, u32[]{:S(2)}) collective-permute-start(bf16[512,256]{1,0:T(8,128)(2,1)S(1)} %pad_maximum_fusion.3.refs_0_), channel_id=1, source_target_pairs={{0,8},{4,12},{8,0},{12,4},{16,24},{20,28},{24,16},{28,20},{1,9},{5... | collective-permute-start | bytes 786440 | tf_op jit(solution)/shard_map/ppermute | solution.py:312
  16.8 5.5 %collective-permute-done.refs_1_ = bf16[512,256]{1,0:T(8,128)(2,1)S(1)} collective-permute-done((bf16[512,256]{1,0:T(8,128)(2,1)S(1)}, bf16[512,256]{1,0:T(8,128)(2,1)S(1)}, u32[]{:S(2)}, u32[]{:S(2)}) %collective-permute-start) | collective-permute-done | bytes 262176 | tf_op jit(solution)/shard_map/ppermute | solution.py:312
  22.3 6.6 %collective-permute-done.1.refs_2_ = bf16[512,256]{1,0:T(8,128)(2,1)S(1)} collective-permute-done((bf16[512,256]{1,0:T(8,128)(2,1)S(1)}, bf16[512,256]{1,0:T(8,128)(2,1)S(1)}, u32[]{:S(2)}, u32[]{:S(2)}) %collective-permute-start.1) | collective-permute-done | bytes 262176 | tf_op jit(solution)/shard_map/ppermute | solution.py:312
  34.4 13.7 %attn_grads.2 = (bf16[512,640]{1,0:T(8,128)(2,1)}, bf16[2048,256]{1,0:T(8,128)(2,1)}, bf16[2048,256]{1,0:T(8,128)(2,1)}) custom-call(s32[4,6]{1,0:T(4,128)} %lists.3, s32[2]{0:T(128)} %globs.3, s32[1]{0:T(128)} %bitcast.here, bf16[512,1280]{1,0:T(8,128)(2,1)} %q_ref.3, bf16[512,1280]{1,0:T(8,128)(2,1)} %do_ref.3, bf16[512,256]{1,0:T(8,128)(2,1)} %copy-done.6, ...), custom_call_target="tpu_custom_call" | custom-call | flops 1000 | bytes 1000 | tf_op jit(solution)/shard_map/attn_grads/pallas_call | solution.py:178
  49.3 2.4 %collective-permute-done.10 = bf16[2048,256]{1,0:T(8,128)(2,1)S(1)} collective-permute-done((bf16[2048,256]{1,0:T(8,128)(2,1)}, bf16[2048,256]{1,0:T(8,128)(2,1)S(1)}, u32[]{:S(2)}, u32[]{:S(2)}) %collective-permute-start.10) | collective-permute-done | bytes 1048608 | tf_op jit(solution)/shard_map/ppermute | solution.py:312
  54.9 4.4 %collective-permute-start.12 = (bf16[512,256]{1,0:T(8,128)(2,1)S(1)}, bf16[512,256]{1,0:T(8,128)(2,1)S(1)}, u32[]{:S(2)}, u32[]{:S(2)}) collective-permute-start(bf16[512,256]{1,0:T(8,128)(2,1)S(1)} %get-tuple-element.60), channel_id=1, source_target_pairs={{0,16},{4,20},{8,24},{12,28},{16,0},{20,4},{24,8},{28,12},{1,17},{... | collective-permute-start | bytes 786440 | tf_op jit(solution)/shard_map/ppermute | solution.py:312
  60.8 13.7 %attn_grads.3 = (bf16[512,640]{1,0:T(8,128)(2,1)}, bf16[2048,256]{1,0:T(8,128)(2,1)}, bf16[2048,256]{1,0:T(8,128)(2,1)}) custom-call(s32[4,6]{1,0:T(4,128)} %lists.3, s32[2]{0:T(128)} %globs.3, s32[1]{0:T(128)} %bitcast.here, bf16[512,1280]{1,0:T(8,128)(2,1)} %q_ref.3, bf16[512,1280]{1,0:T(8,128)(2,1)} %do_ref.3, bf16[512,256]{1,0:T(8,128)(2,1)} %copy-done.5, ...), custom_call_target="tpu_custom_call" | custom-call | flops 1000 | bytes 1000 | tf_op jit(solution)/shard_map/attn_grads/pallas_call | solution.py:178
  76.0 3.3 %collective-permute-done.18 = bf16[2048,256]{1,0:T(8,128)(2,1)S(1)} collective-permute-done((bf16[2048,256]{1,0:T(8,128)(2,1)}, bf16[2048,256]{1,0:T(8,128)(2,1)S(1)}, u32[]{:S(2)}, u32[]{:S(2)}) %collective-permute-start.18) | collective-permute-done | bytes 1048608 | tf_op jit(solution)/shard_map/ppermute | solution.py:312
  79.6 1.6 collective-permute-start.23
  81.2 5.7 %collective-permute-start.22 = (bf16[512,256]{1,0:T(8,128)(2,1)S(1)}, bf16[512,256]{1,0:T(8,128)(2,1)S(1)}, u32[]{:S(2)}, u32[]{:S(2)}) collective-permute-start(bf16[512,256]{1,0:T(8,128)(2,1)S(1)} %get-tuple-element.56), channel_id=1, source_target_pairs={{0,16},{4,20},{8,24},{12,28},{16,0},{20,4},{24,8},{28,12},{1,17},{... | collective-permute-start | bytes 786440 | tf_op jit(solution)/shard_map/ppermute | solution.py:312
  86.9 13.0 %query_term.1.refs_2_ = bf16[512,5120]{1,0:T(8,128)(2,1)} custom-call(bf16[512,640]{1,0:T(8,128)(2,1)} %get-tuple-element.36.refs_0_, bf16[512,640]{1,0:T(8,128)(2,1)} %get-tuple-element.35.refs_1_, bf16[5120,1280]{1,0:T(8,128)(2,1)} %refs_2_.1), custom_call_target="tpu_custom_call" | custom-call | flops 1000 | bytes 1000 | tf_op jit(solution)/shard_map/query_term/pallas_call | solution.py:226
  100.7 8.5 %kv_term.1 = bf16[512,5120]{1,0:T(8,128)(2,1)} custom-call(bf16[512,256]{1,0:T(8,128)(2,1)} %add_convert_fusion.3.refs_0_, bf16[512,256]{1,0:T(8,128)(2,1)} %add_convert_fusion.2.refs_1_, bf16[512,5120]{1,0:T(8,128)(2,1)} %query_term.1.refs_2_, bf16[5120,256]{1,0:T(8,128)(2,1)} %refs_3_.1, bf16[5120,256]{1,0:T(8,128)(2,1)} %refs_4_.1), custom_call_target="tpu_custom_call" | custom-call | flops 1000 | bytes 1000 | tf_op jit(solution)/shard_map/kv_term/pallas_call | solution.py:260
  109.3 3.6 %all-gather.3.cloned.1.call-done = bf16[4096,640]{1,0:T(8,128)(2,1)} async-done(((bf16[1024,640]{1,0:T(8,128)(2,1)}), bf16[4096,640]{1,0:T(8,128)(2,1)}) %all-gather.3.cloned.1.call-update) | async-done | bytes 5242896 | tf_op jit(solution)/shard_map/all_gather | solution.py:377
  112.9 12.3 %weight_grad.2 = bf16[4,640,1280]{2,1,0:T(8,128)(2,1)} custom-call(s32[1]{0:T(128)} %bitcast.1.chip, bf16[4,1024,640]{2,1,0:T(8,128)(2,1)} %bitcast.59, bf16[512,640]{1,0:T(8,128)(2,1)} %get-tuple-element.36.refs_0_, bf16[512,640]{1,0:T(8,128)(2,1)} %get-tuple-element.35.refs_1_, bf16[512,640]{1,0:T(8,128)(2,1)} %copy-done.7, bf16[512,640]{1,0:T(8,128)(2,1)} %copy-done.8), custom_call_target="tpu_custom_call" | custom-call | flops 1000 | bytes 1000 | tf_op jit(solution)/shard_map/weight_grad/pallas_call | solution.py:293
  125.2 2.2 slice_bitcast_fusion.6
  132.8 6.8 %weight_grad.3 = bf16[4,640,512]{2,1,0:T(8,128)(2,1)} custom-call(s32[1]{0:T(128)} %bitcast.1.chip, bf16[4,1024,640]{2,1,0:T(8,128)(2,1)} %bitcast.60, bf16[512,256]{1,0:T(8,128)(2,1)} %add_convert_fusion.3.refs_0_, bf16[512,256]{1,0:T(8,128)(2,1)} %add_convert_fusion.2.refs_1_, bf16[512,256]{1,0:T(8,128)(2,1)} %copy-done.23, bf16[512,256]{1,0:T(8,128)(2,1)} %copy-done.24), custom_call_target="tpu_custom_call" | custom-call | flops 1000 | bytes 1000 | tf_op jit(solution)/shard_map/weight_grad/pallas_call | solution.py:293
  143.2 5.3 %collective-permute-done.26 = bf16[320,1280]{1,0:T(8,128)(2,1)S(1)} collective-permute-done((bf16[320,1280]{1,0:T(8,128)(2,1)S(1)}, bf16[320,1280]{1,0:T(8,128)(2,1)S(1)}, u32[]{:S(2)}, u32[]{:S(2)}) %collective-permute-start.26) | collective-permute-done | bytes 819232 | tf_op jit(solution)/shard_map/ppermute | solution.py:312
  151.3 12.6 %collective-permute-done.36 = bf16[320,512]{1,0:T(8,128)(2,1)S(1)} collective-permute-done((bf16[320,512]{1,0:T(8,128)(2,1)S(1)}, bf16[320,512]{1,0:T(8,128)(2,1)S(1)}, u32[]{:S(2)}, u32[]{:S(2)}) %collective-permute-start.36) | collective-permute-done | bytes 327712 | tf_op jit(solution)/shard_map/ppermute | solution.py:312
  167.0 6.0 %collective-permute-done.34 = bf16[320,512]{1,0:T(8,128)(2,1)S(1)} collective-permute-done((bf16[320,512]{1,0:T(8,128)(2,1)S(1)}, bf16[320,512]{1,0:T(8,128)(2,1)S(1)}, u32[]{:S(2)}, u32[]{:S(2)}) %collective-permute-start.34) | collective-permute-done | bytes 327712 | tf_op jit(solution)/shard_map/ppermute | solution.py:312
  174.6 4.6 %collective-permute-done.37 = bf16[320,512]{1,0:T(8,128)(2,1)S(1)} collective-permute-done((bf16[320,512]{1,0:T(8,128)(2,1)S(1)}, bf16[320,512]{1,0:T(8,128)(2,1)S(1)}, u32[]{:S(2)}, u32[]{:S(2)}) %collective-permute-start.37) | collective-permute-done | bytes 327712 | tf_op jit(solution)/shard_map/ppermute | solution.py:312
  182.4 2.7 %collective-permute-done.27 = bf16[320,1280]{1,0:T(8,128)(2,1)S(1)} collective-permute-done((bf16[320,1280]{1,0:T(8,128)(2,1)S(1)}, bf16[320,1280]{1,0:T(8,128)(2,1)S(1)}, u32[]{:S(2)}, u32[]{:S(2)}) %collective-permute-start.27) | collective-permute-done | bytes 819232 | tf_op jit(solution)/shard_map/ppermute | solution.py:312
  185.1 2.1 fusion.5
  189.8 17.9 %collective-permute-done.35 = bf16[320,512]{1,0:T(8,128)(2,1)S(1)} collective-permute-done((bf16[320,512]{1,0:T(8,128)(2,1)S(1)}, bf16[320,512]{1,0:T(8,128)(2,1)S(1)}, u32[]{:S(2)}, u32[]{:S(2)}) %collective-permute-start.35) | collective-permute-done | bytes 327712 | tf_op jit(solution)/shard_map/ppermute | solution.py:312
  (143 shorter events, 45.4 us)
Async XLA Ops:
  7.2 105.7 %all-gather.3.cloned.1.call-start = ((), (), s32[]{:S(2)}) async-start(), calls=%async_computation.2 | async-start | bytes 6553600 | tf_op jit(solution)/shard_map/all_gather | solution.py:377
  12.1 200.1 %reduce-scatter.2.cloned.1.call-start = ((), (), s32[]{:S(2)}) async-start(), calls=%async_computation.1 | async-start | bytes 6553600 | tf_op jit(solution)/shard_map/reduce_scatter | solution.py:412
  15.2 13.7 %collective-permute-start.1 = (bf16[512,256]{1,0:T(8,128)(2,1)S(1)}, bf16[512,256]{1,0:T(8,128)(2,1)S(1)}, u32[]{:S(2)}, u32[]{:S(2)}) collective-permute-start(bf16[512,256]{1,0:T(8,128)(2,1)S(1)} %pad_maximum_fusion.3.refs_0_), channel_id=1, source_target_pairs={{0,16},{4,20},{8,24},{12,28},{16,0},{20,4},{24,8},{28,12},{1,17},{... | collective-permute-start | bytes 786440 | tf_op jit(solution)/shard_map/ppermute | solution.py:312
  16.8 12.7 %collective-permute-start.3 = (bf16[512,256]{1,0:T(8,128)(2,1)S(1)}, bf16[512,256]{1,0:T(8,128)(2,1)S(1)}, u32[]{:S(2)}, u32[]{:S(2)}) collective-permute-start(bf16[512,256]{1,0:T(8,128)(2,1)S(1)} %pad_maximum_fusion.3.refs_0_), channel_id=1, source_target_pairs={{0,4},{4,0},{8,12},{12,8},{16,20},{20,16},{24,28},{28,24},{1,5},{5... | collective-permute-start | bytes 786440 | tf_op jit(solution)/shard_map/ppermute | solution.py:312
  30.8 17.3 %collective-permute-start.7 = (bf16[512,256]{1,0:T(8,128)(2,1)S(1)}, bf16[512,256]{1,0:T(8,128)(2,1)S(1)}, u32[]{:S(2)}, u32[]{:S(2)}) collective-permute-start(bf16[512,256]{1,0:T(8,128)(2,1)S(1)} %pad_maximum_fusion.4.refs_0_), channel_id=1, source_target_pairs={{0,8},{4,12},{8,0},{12,4},{16,24},{20,28},{24,16},{28,20},{1,9},{5... | collective-permute-start | bytes 786440 | tf_op jit(solution)/shard_map/ppermute | solution.py:312
  31.7 16.4 %collective-permute-start.8 = (bf16[512,256]{1,0:T(8,128)(2,1)S(1)}, bf16[512,256]{1,0:T(8,128)(2,1)S(1)}, u32[]{:S(2)}, u32[]{:S(2)}) collective-permute-start(bf16[512,256]{1,0:T(8,128)(2,1)S(1)} %pad_maximum_fusion.4.refs_0_), channel_id=1, source_target_pairs={{0,16},{4,20},{8,24},{12,28},{16,0},{20,4},{24,8},{28,12},{1,17},{... | collective-permute-start | bytes 786440 | tf_op jit(solution)/shard_map/ppermute | solution.py:312
  32.9 15.3 %collective-permute-start.9 = (bf16[512,256]{1,0:T(8,128)(2,1)S(1)}, bf16[512,256]{1,0:T(8,128)(2,1)S(1)}, u32[]{:S(2)}, u32[]{:S(2)}) collective-permute-start(bf16[512,256]{1,0:T(8,128)(2,1)S(1)} %pad_maximum_fusion.4.refs_0_), channel_id=1, source_target_pairs={{0,24},{4,28},{8,16},{12,20},{16,8},{20,12},{24,0},{28,4},{1,25},{... | collective-permute-start | bytes 786440 | tf_op jit(solution)/shard_map/ppermute | solution.py:312
  53.4 21.2 %collective-permute-start.13 = (bf16[512,256]{1,0:T(8,128)(2,1)S(1)}, bf16[512,256]{1,0:T(8,128)(2,1)S(1)}, u32[]{:S(2)}, u32[]{:S(2)}) collective-permute-start(bf16[512,256]{1,0:T(8,128)(2,1)S(1)} %get-tuple-element.59), channel_id=1, source_target_pairs={{0,24},{4,28},{8,16},{12,20},{16,8},{20,12},{24,0},{28,4},{1,25},{... | collective-permute-start | bytes 786440 | tf_op jit(solution)/shard_map/ppermute | solution.py:312
  54.9 19.7 %collective-permute-start.12 = (bf16[512,256]{1,0:T(8,128)(2,1)S(1)}, bf16[512,256]{1,0:T(8,128)(2,1)S(1)}, u32[]{:S(2)}, u32[]{:S(2)}) collective-permute-start(bf16[512,256]{1,0:T(8,128)(2,1)S(1)} %get-tuple-element.60), channel_id=1, source_target_pairs={{0,16},{4,20},{8,24},{12,28},{16,0},{20,4},{24,8},{28,12},{1,17},{... | collective-permute-start | bytes 786440 | tf_op jit(solution)/shard_map/ppermute | solution.py:312
  59.3 15.3 %collective-permute-start.11 = (bf16[512,256]{1,0:T(8,128)(2,1)S(1)}, bf16[512,256]{1,0:T(8,128)(2,1)S(1)}, u32[]{:S(2)}, u32[]{:S(2)}) collective-permute-start(bf16[512,256]{1,0:T(8,128)(2,1)S(1)} %get-tuple-element.61), channel_id=1, source_target_pairs={{0,8},{4,12},{8,0},{12,4},{16,24},{20,28},{24,16},{28,20},{1,9},{5... | collective-permute-start | bytes 786440 | tf_op jit(solution)/shard_map/ppermute | solution.py:312
  79.6 20.3 %collective-permute-start.23 = (bf16[512,256]{1,0:T(8,128)(2,1)S(1)}, bf16[512,256]{1,0:T(8,128)(2,1)S(1)}, u32[]{:S(2)}, u32[]{:S(2)}) collective-permute-start(bf16[512,256]{1,0:T(8,128)(2,1)S(1)} %get-tuple-element.55), channel_id=1, source_target_pairs={{0,24},{4,28},{8,16},{12,20},{16,8},{20,12},{24,0},{28,4},{1,25},{... | collective-permute-start | bytes 786440 | tf_op jit(solution)/shard_map/ppermute | solution.py:312
  81.2 18.7 %collective-permute-start.22 = (bf16[512,256]{1,0:T(8,128)(2,1)S(1)}, bf16[512,256]{1,0:T(8,128)(2,1)S(1)}, u32[]{:S(2)}, u32[]{:S(2)}) collective-permute-start(bf16[512,256]{1,0:T(8,128)(2,1)S(1)} %get-tuple-element.56), channel_id=1, source_target_pairs={{0,16},{4,20},{8,24},{12,28},{16,0},{20,4},{24,8},{28,12},{1,17},{... | collective-permute-start | bytes 786440 | tf_op jit(solution)/shard_map/ppermute | solution.py:312
  86.9 13.0 %collective-permute-start.21 = (bf16[512,256]{1,0:T(8,128)(2,1)S(1)}, bf16[512,256]{1,0:T(8,128)(2,1)S(1)}, u32[]{:S(2)}, u32[]{:S(2)}) collective-permute-start(bf16[512,256]{1,0:T(8,128)(2,1)S(1)} %get-tuple-element.57), channel_id=1, source_target_pairs={{0,8},{4,12},{8,0},{12,4},{16,24},{20,28},{24,16},{28,20},{1,9},{5... | collective-permute-start | bytes 786440 | tf_op jit(solution)/shard_map/ppermute | solution.py:312
  127.3 21.2 %collective-permute-start.26 = (bf16[320,1280]{1,0:T(8,128)(2,1)S(1)}, bf16[320,1280]{1,0:T(8,128)(2,1)S(1)}, u32[]{:S(2)}, u32[]{:S(2)}) collective-permute-start(bf16[320,1280]{1,0:T(8,128)(2,1)S(1)} %get-tuple-element.45), channel_id=1, source_target_pairs={{0,8},{4,12},{8,0},{12,4},{16,24},{20,28},{24,16},{28,20},{1,9},{5... | collective-permute-start | bytes 2457608 | tf_op jit(solution)/shard_map/ppermute | solution.py:312
  129.4 51.5 %collective-permute-start.25 = (bf16[320,1280]{1,0:T(8,128)(2,1)S(1)}, bf16[320,1280]{1,0:T(8,128)(2,1)S(1)}, u32[]{:S(2)}, u32[]{:S(2)}) collective-permute-start(bf16[320,1280]{1,0:T(8,128)(2,1)S(1)} %get-tuple-element.42), channel_id=1, source_target_pairs={{0,8},{4,12},{8,0},{12,4},{16,24},{20,28},{24,16},{28,20},{1,9},{5... | collective-permute-start | bytes 2457608 | tf_op jit(solution)/shard_map/ppermute | solution.py:312
  129.9 52.5 %collective-permute-start.28 = (bf16[320,1280]{1,0:T(8,128)(2,1)S(1)}, bf16[320,1280]{1,0:T(8,128)(2,1)}, u32[]{:S(2)}, u32[]{:S(2)}) collective-permute-start(bf16[320,1280]{1,0:T(8,128)(2,1)S(1)} %get-tuple-element.44), channel_id=1, source_target_pairs={{0,16},{4,20},{8,24},{12,28},{16,0},{20,4},{24,8},{28,12},{1,17},{... | collective-permute-start | bytes 2457608 | tf_op jit(solution)/shard_map/ppermute | solution.py:312
  141.1 24.4 %collective-permute-start.38 = (bf16[320,512]{1,0:T(8,128)(2,1)S(1)}, bf16[320,512]{1,0:T(8,128)(2,1)S(1)}, u32[]{:S(2)}, u32[]{:S(2)}) collective-permute-start(bf16[320,512]{1,0:T(8,128)(2,1)S(1)} %get-tuple-element.49), channel_id=1, source_target_pairs={{0,16},{4,20},{8,24},{12,28},{16,0},{20,4},{24,8},{28,12},{1,17},{... | collective-permute-start | bytes 983048 | tf_op jit(solution)/shard_map/ppermute | solution.py:312
  141.7 22.2 %collective-permute-start.36 = (bf16[320,512]{1,0:T(8,128)(2,1)S(1)}, bf16[320,512]{1,0:T(8,128)(2,1)S(1)}, u32[]{:S(2)}, u32[]{:S(2)}) collective-permute-start(bf16[320,512]{1,0:T(8,128)(2,1)S(1)} %get-tuple-element.48), channel_id=1, source_target_pairs={{0,16},{4,20},{8,24},{12,28},{16,0},{20,4},{24,8},{28,12},{1,17},{... | collective-permute-start | bytes 983048 | tf_op jit(solution)/shard_map/ppermute | solution.py:312
  148.5 24.6 %collective-permute-start.34 = (bf16[320,512]{1,0:T(8,128)(2,1)S(1)}, bf16[320,512]{1,0:T(8,128)(2,1)S(1)}, u32[]{:S(2)}, u32[]{:S(2)}) collective-permute-start(bf16[320,512]{1,0:T(8,128)(2,1)S(1)} %get-tuple-element.50), channel_id=1, source_target_pairs={{0,8},{4,12},{8,0},{12,4},{16,24},{20,28},{24,16},{28,20},{1,9},{5... | collective-permute-start | bytes 983048 | tf_op jit(solution)/shard_map/ppermute | solution.py:312
  163.9 21.2 %collective-permute-start.27 = (bf16[320,1280]{1,0:T(8,128)(2,1)S(1)}, bf16[320,1280]{1,0:T(8,128)(2,1)S(1)}, u32[]{:S(2)}, u32[]{:S(2)}) collective-permute-start(bf16[320,1280]{1,0:T(8,128)(2,1)S(1)} %fusion.3), channel_id=1, source_target_pairs={{0,16},{4,20},{8,24},{12,28},{16,0},{20,4},{24,8},{28,12},{1,17},{... | collective-permute-start | bytes 2457608 | tf_op jit(solution)/shard_map/ppermute | solution.py:312
  165.5 13.6 %collective-permute-start.37 = (bf16[320,512]{1,0:T(8,128)(2,1)S(1)}, bf16[320,512]{1,0:T(8,128)(2,1)S(1)}, u32[]{:S(2)}, u32[]{:S(2)}) collective-permute-start(bf16[320,512]{1,0:T(8,128)(2,1)S(1)} %fusion.8), channel_id=1, source_target_pairs={{0,8},{4,12},{8,0},{12,4},{16,24},{20,28},{24,16},{28,20},{1,9},{5... | collective-permute-start | bytes 983048 | tf_op jit(solution)/shard_map/ppermute | solution.py:312
  173.1 36.3 %collective-permute-start.30 = (bf16[320,1280]{1,0:T(8,128)(2,1)S(1)}, bf16[320,1280]{1,0:T(8,128)(2,1)S(1)}, u32[]{:S(2)}, u32[]{:S(2)}) collective-permute-start(bf16[320,1280]{1,0:T(8,128)(2,1)S(1)} %get-tuple-element.43), channel_id=1, source_target_pairs={{0,16},{4,20},{8,24},{12,28},{16,0},{20,4},{24,8},{28,12},{1,17},{... | collective-permute-start | bytes 2457608 | tf_op jit(solution)/shard_map/ppermute | solution.py:312
  180.8 26.8 %collective-permute-start.35 = (bf16[320,512]{1,0:T(8,128)(2,1)S(1)}, bf16[320,512]{1,0:T(8,128)(2,1)S(1)}, u32[]{:S(2)}, u32[]{:S(2)}) collective-permute-start(bf16[320,512]{1,0:T(8,128)(2,1)S(1)} %get-tuple-element.47), channel_id=1, source_target_pairs={{0,16},{4,20},{8,24},{12,28},{16,0},{20,4},{24,8},{28,12},{1,17},{... | collective-permute-start | bytes 983048 | tf_op jit(solution)/shard_map/ppermute | solution.py:312
  187.2 22.2 %collective-permute-start.29 = (bf16[320,1280]{1,0:T(8,128)(2,1)S(1)}, bf16[320,1280]{1,0:T(8,128)(2,1)S(1)}, u32[]{:S(2)}, u32[]{:S(2)}) collective-permute-start(bf16[320,1280]{1,0:T(8,128)(2,1)S(1)} %get-tuple-element.41), channel_id=1, source_target_pairs={{0,8},{4,12},{8,0},{12,4},{16,24},{20,28},{24,16},{28,20},{1,9},{5... | collective-permute-start | bytes 2457608 | tf_op jit(solution)/shard_map/ppermute | solution.py:312
  (44 other events, 305.4 us)
Sparse Core Ops, SparseCore 0:
  12.2 100.6 all-gather.2
  115.8 92.1 reduce-scatter.1
